TPU v7x, 32 devices: a whole 2x2x4 slice. The times are simulated.
32 devices in a mesh: segment: 4 (over y, core), vol: 8 (over z, x).
Axes of the slice: x: 2, y: 2, z: 4, core: 2. Of those that a mesh axis runs over, the one named last changes fastest.
Arguments:
- cotangent: bfloat16 [64, 32, 256], P(None, 'vol'), may hold values from -6 to 6
- labels: int32 [32, 256], P('vol'), may hold values from 0 to 2
- class_weight: float32 [3], replicated, may hold values from 0.25 to 2
- inputs: bfloat16 [4, 64, 32, 256], P('segment', None, 'vol'), may hold values from -6 to 6
- fine_pre: bfloat16 [4, 64, 32, 256], P('segment', None, 'vol'), may hold values from -6 to 6
- pooled: bfloat16 [4, 64, 8, 128], P('segment', None, 'vol'), may hold values from -6 to 6
- coarse_pre: bfloat16 [4, 64, 8, 128], P('segment', None, 'vol'), may hold values from -6 to 6
- fine_filters: bfloat16 [4, 27, 64, 64], P('segment'), may hold values from -0.15625 to 0.15625
- coarse_filters: bfloat16 [4, 27, 64, 64], P('segment'), may hold values from -0.15625 to 0.15625
Outputs:
- input_grads: bfloat16 [4, 64, 32, 256], P('segment', None, 'vol')
- fine_filter_grads: float32 [4, 27, 64, 64], P('segment')
- coarse_filter_grads: float32 [4, 27, 64, 64], P('segment')
Inputs may be any that keep to these rules, and one draw needn't show every extreme that they name: `labels`: 0 is background, 1 fault, 2 horizon.
All inputs are finite; a program needn't handle non-finite values.
Results may differ from a plain program's by a relative error of at most 0.02.
Values may be sent and summed in bfloat16 or wider, within the bound.
A program may use at most 64 MiB of HBM per device.

v0:
```python
import functools
import math

import jax
import jax.numpy as jnp
from jax import lax
from jax.experimental import pallas as pl
from jax.experimental.pallas import tpu as pltpu
from jax.sharding import PartitionSpec as P

XL = 16
HX = XL // 2
TAPS = 27
BF = jnp.bfloat16
F32 = jnp.float32


def iota(shape, dim):
    return lax.broadcasted_iota(jnp.int32, shape, dim)


def matmul(a, b):
    return lax.dot_general(a, b, (((1,), (0,)), ((), ())), preferred_element_type=F32)


def matmul_nt(a, b):
    return lax.dot_general(a, b, (((1,), (1,)), ((), ())), preferred_element_type=F32)


def tap_mask(lanes, plane, columns, row_step, col_step):
    lane = iota((1, lanes), 1)
    column = lax.rem(lane, columns) - col_step
    row = lax.div(lax.rem(lane, plane), columns) - row_step
    rows = plane // columns
    inside = (column >= 0) & (column < columns) & (row >= 0) & (row < rows)
    return jnp.where(inside, 1.0, 0.0).astype(BF)


def rolled(value, shift):
    size = value.shape[1]
    shift = shift % size
    return value if shift == 0 else pltpu.roll(value, shift, 1)


def kernel(
    sizes,
    class_weight, cotangent, labels, saved, fine_pre, coarse_pre, pooled, fine_w, coarse_w,
    out, collected,
    seed, fine_cat, coarse_cat, pre_rows, pool_rows, pre_ext, grad_ext, pool_ext, pool_out,
    coarse_gate, fine_x, coarse_x, fine_cols, coarse_cols, parts, arrived,
    row_send, row_recv, halo_send, halo_recv, step_send, step_recv, sum_send, sum_recv,
    all_send, all_recv,
):
    segments, n, channels, depth, plane, per, chunks = sizes
    cw = plane // 4
    cdepth = depth // 2
    own = depth * plane
    row_len = coarse_pre.shape[1]
    s = lax.axis_index("segment")
    v = lax.axis_index("vol")
    has_left, has_right = v > 0, v < n - 1
    last = s == segments - 1

    def put(src, dst, send, recv, segment, vol):
        return pltpu.make_async_remote_copy(
            src_ref=src, dst_ref=dst, send_sem=send, recv_sem=recv,
            device_id=(segment, vol), device_id_type=pl.DeviceIdType.MESH,
        )

    barrier = pltpu.get_barrier_semaphore()

    def greet(off, carry):
        pl.semaphore_signal(
            barrier, inc=1, device_id=(s, lax.rem(v + off, n)),
            device_id_type=pl.DeviceIdType.MESH,
        )
        return carry

    lax.fori_loop(1, n, greet, 0)
    for up in (-1, 1):
        for side in (-1, 0, 1):
            there = (s + up >= 0) & (s + up < segments) & (v + side >= 0) & (v + side < n)

            @pl.when(there)
            def _(up=up, side=side):
                pl.semaphore_signal(
                    barrier, inc=1, device_id=(s + up, v + side),
                    device_id_type=pl.DeviceIdType.MESH,
                )

    ups = jnp.where(s > 0, 1, 0) + jnp.where(last, 0, 1)
    sides = 1 + jnp.where(has_left, 1, 0) + jnp.where(has_right, 1, 0)
    pl.semaphore_wait(barrier, n - 1 + ups * sides)

    to_left = put(
        pre_ext.at[1], pre_ext.at[depth + 1],
        halo_send.at[0], halo_recv.at[0], s, v - 1,
    )
    to_right = put(
        pre_ext.at[depth], pre_ext.at[0],
        halo_send.at[1], halo_recv.at[1], s, v + 1,
    )

    def row_copy(which, off):
        src, dst = ((coarse_pre, pre_rows), (pooled, pool_rows))[which]
        return put(
            src, dst.at[v], row_send.at[which, off], row_recv.at[which, v],
            s, lax.rem(v + off, n),
        )

    def send_rows(which):
        def body(off, carry):
            row_copy(which, off).start()
            return carry

        lax.fori_loop(1, n, body, 0)

    def wait_rows(which):
        src, dst = ((coarse_pre, pre_rows), (pooled, pool_rows))[which]

        def body(off, carry):
            u = lax.rem(v + off, n)
            put(src, dst.at[u], row_send.at[which, off], row_recv.at[which, u], s, u).wait_recv()
            return carry

        lax.fori_loop(1, n, body, 0)

    fine_lane = iota((1, own), 1)
    pool_target = (
        lax.div(fine_lane, 2 * plane) * cw
        + lax.div(lax.rem(fine_lane, plane), 2 * XL) * HX
        + lax.div(lax.rem(fine_lane, XL), 2)
    )
    pool_matrix = jnp.where(iota((cdepth * cw, own), 0) == pool_target, 1.0, 0.0).astype(BF)

    def step_copies(src, turn, segment):
        def step(which, a, b, vol):
            return put(a, b, step_send.at[turn, which], step_recv.at[which], segment, vol)

        block = pool_out.at[turn]
        return (
            step(0, src, grad_ext.at[1:depth + 1], v),
            step(1, src.at[0], grad_ext.at[depth + 1], v - 1),
            step(2, src.at[depth - 1], grad_ext.at[0], v + 1),
            step(3, block, pool_ext.at[1], v),
            step(4, block, pool_ext.at[2], v - 1),
            step(5, block, pool_ext.at[0], v + 1),
        )

    def guarded(copies, act, with_own):
        @pl.when(has_left)
        def _():
            act(copies[4])

        @pl.when(has_right)
        def _():
            act(copies[5])

        if with_own:
            act(copies[3])

        @pl.when(has_left)
        def _():
            act(copies[1])

        @pl.when(has_right)
        def _():
            act(copies[2])

        if with_own:
            act(copies[0])

    def joined(ref):
        return jnp.concatenate([ref[p] for p in range(depth)], axis=1)

    send_rows(0)

    @pl.when(last)
    def _():
        planes = jnp.swapaxes(cotangent[...], 0, 1)
        for p in range(depth):
            label = labels[p:p + 1, :]
            weight = jnp.zeros(label.shape, F32)
            for index in range(class_weight.shape[0]):
                weight = weight + jnp.where(label == index, class_weight[index], 0.0)
            block = (planes[p].astype(F32) * weight).astype(BF)
            seed[p] = block
            grad_ext[p + 1] = block
        pool_out[0] = matmul_nt(joined(seed), pool_matrix).astype(BF)
        guarded(step_copies(seed, 0, s), lambda c: c.start(), False)
        pool_ext[1] = pool_out[0]

    pre_ext[1:depth + 1] = jnp.swapaxes(fine_pre[...], 0, 1)

    @pl.when(has_left)
    def _():
        to_left.start()

    @pl.when(has_right)
    def _():
        to_right.start()

    for k in range(TAPS):
        rows = slice(k // 9 * channels, (k // 9 + 1) * channels)
        lanes = slice(k % 9 * channels, (k % 9 + 1) * channels)
        coarse_cat[rows, lanes] = coarse_w[k]
        fine_cat[rows, lanes] = fine_w[k]
    planes = jnp.swapaxes(saved[...], 0, 1)
    for outer in range(3):
        rows = slice(outer * channels, (outer + 1) * channels)
        for p in range(depth + 2):
            q = p - 2 + outer
            block = planes[q] if 0 <= q < depth else jnp.zeros((channels, plane), BF)
            fine_x[rows, p * plane:(p + 1) * plane] = block
    pre_rows[v] = coarse_pre[...]
    pool_rows[v] = pooled[...]

    @pl.when(v == 0)
    def _():
        pre_ext[0] = jnp.zeros((channels, plane), BF)
        grad_ext[0] = jnp.zeros((channels, plane), BF)
        pool_ext[0] = jnp.zeros(pool_ext.shape[1:], BF)

    @pl.when(v == n - 1)
    def _():
        pre_ext[depth + 1] = jnp.zeros((channels, plane), BF)
        grad_ext[depth + 1] = jnp.zeros((channels, plane), BF)
        pool_ext[2] = jnp.zeros(pool_ext.shape[1:], BF)

    up_lane = iota((1, plane), 1)
    up_target = lax.div(up_lane, 2 * XL) * HX + lax.div(lax.rem(up_lane, XL), 2)
    up_matrix = jnp.where(iota((cw, plane), 0) == up_target, 0.125, 0.0).astype(BF)

    def gathered(rows, first, planes, low, high):
        lane = iota((1, planes * cw), 1)
        slab = lax.div(lane, cw)
        target = (first + slab) * HX + lax.rem(lane, HX)
        target = jnp.where((slab >= low) & (slab < high), target, -1)
        inline = lax.div(lax.rem(lane, cw), HX)
        row = iota((row_len, planes * cw), 0)

        def body(u, total):
            pick = jnp.where(row == jnp.where(inline == u, target, -1), 1.0, 0.0).astype(BF)
            return total + matmul(rows[u], pick)

        return lax.fori_loop(0, n, body, jnp.zeros((channels, planes * cw), F32))

    wait_rows(0)
    send_rows(1)
    reach = cdepth + 4
    coarse_gate[...] = gathered(pre_rows, v * cdepth - 2, reach, 0, reach).astype(BF)

    def take_pooled():
        wait_rows(1)
        own_x = gathered(pool_rows, v * cdepth - 2, reach, 2, 2 + cdepth).astype(BF)
        for outer in range(3):
            coarse_x[outer * channels:(outer + 1) * channels, :] = rolled(own_x, (1 - outer) * cw)

    @pl.when(jnp.logical_not(last))
    def _():
        take_pooled()

    incoming = step_copies(out, 1, s)

    def wait_incoming(middle, left, right):
        @pl.when(jnp.logical_not(last))
        def _():
            incoming[middle].wait_recv()

        @pl.when(has_left)
        def _():
            incoming[left].wait_recv()

        @pl.when(has_right)
        def _():
            incoming[right].wait_recv()

    wait_incoming(3, 5, 4)

    def place(which, k, value):
        at = (k % per) * channels
        parts[which, k // per, :, at:at + channels] = value

    def chunk_of(which, vol):
        return vol if which == 0 else n - 1 - vol

    def sum_copy(which, off, vol_from, vol_to, chunk):
        return put(
            parts.at[which, chunk], arrived.at[which, vol_from],
            sum_send.at[which, off], sum_recv.at[which, vol_from], s, vol_to,
        )

    def start_sums(which):
        for k in range(TAPS, chunks * per):
            place(which, k, jnp.zeros((channels, channels), BF))

        def body(off, carry):
            t = lax.rem(v + off, n)
            chunk = chunk_of(which, t)

            @pl.when(chunk < chunks)
            def _():
                sum_copy(which, off, v, t, chunk).start()

            return carry

        lax.fori_loop(1, n, body, 0)

    def place_all(which, grads):
        for k in range(TAPS):
            rows = slice(k // 9 * channels, (k // 9 + 1) * channels)
            place(which, k, grads[rows, k % 9 * channels:(k % 9 + 1) * channels])
        start_sums(which)

    def fine_sums():
        place_all(0, matmul_nt(fine_x[...], fine_cols[...]).astype(BF))

    def coarse_sums():
        place_all(1, matmul_nt(coarse_x[...], coarse_cols[...]).astype(BF))

    side = pool_ext.shape[2]
    near = jnp.concatenate(
        [pool_ext[0][:, side - 2 * cw:], pool_ext[1], pool_ext[2][:, :2 * cw]], axis=1
    )
    coarse_gz = jnp.where(coarse_gate[...] > 0, near, jnp.zeros_like(near))
    for row_step in (-1, 0, 1):
        for col_step in (-1, 0, 1):
            mask = tap_mask(reach * cw, cw, HX, row_step, col_step)
            r = (row_step + 1) * 3 + col_step + 1
            coarse_cols[r * channels:(r + 1) * channels, :] = (
                rolled(coarse_gz, row_step * HX + col_step) * mask
            )

    @pl.when(s == 0)
    def _():
        coarse_sums()

    def over_depth(terms, step, width):
        return sum(
            terms[outer * channels:(outer + 1) * channels, (2 - outer) * step:(2 - outer) * step + width]
            for outer in range(3)
        )

    terms = matmul(coarse_cat[...], coarse_cols[...])
    coarse_back = over_depth(terms, cw, (cdepth + 2) * cw).astype(BF)

    pieces = []
    for p in range(depth + 2):
        j = (p + 1) // 2
        if p and j == p // 2:
            spread = pieces[-1]
        else:
            spread = matmul(coarse_back[:, j * cw:(j + 1) * cw], up_matrix)
        pieces.append(spread)

    @pl.when(has_left)
    def _():
        to_right.wait_recv()

    @pl.when(has_right)
    def _():
        to_left.wait_recv()

    wait_incoming(0, 2, 1)
    gz = []
    for p in range(depth + 2):
        grad = grad_ext[p].astype(F32) + pieces[p]
        gz.append(jnp.where(pre_ext[p].astype(F32) > 0, grad, 0.0).astype(BF))
    for row_step in (-1, 0, 1):
        for col_step in (-1, 0, 1):
            mask = tap_mask(plane, plane, XL, row_step, col_step)
            r = (row_step + 1) * 3 + col_step + 1
            for p in range(depth + 2):
                fine_cols[r * channels:(r + 1) * channels, p * plane:(p + 1) * plane] = (
                    rolled(gz[p], row_step * XL + col_step) * mask
                )
    @pl.when(s == 0)
    def _():
        fine_sums()

    total = over_depth(matmul(fine_cat[...], fine_cols[...]), plane, own)
    total = total + jnp.concatenate([grad_ext[p + 1].astype(F32) for p in range(depth)], axis=1)
    for p in range(depth):
        out[p] = total[:, p * plane:(p + 1) * plane].astype(BF)

    @pl.when(s > 0)
    def _():
        pool_out[1] = matmul_nt(joined(out), pool_matrix).astype(BF)
        guarded(step_copies(out, 1, s - 1), lambda c: c.start(), True)

    @pl.when(s > 0)
    def _():
        fine_sums()

        @pl.when(last)
        def _():
            take_pooled()

        coarse_sums()

    def all_copy(which, off, chunk, vol_to):
        return put(
            collected.at[which, chunk], collected.at[which, chunk],
            all_send.at[which, off], all_recv.at[which, chunk], s, vol_to,
        )

    for which in (1, 0):
        mine = chunk_of(which, v)

        @pl.when(mine < chunks)
        def _(which=which, mine=mine):
            def add(off, carry):
                u = lax.rem(v + off, n)
                sum_copy(which, off, u, u, mine).wait_recv()
                return carry + arrived[which, u].astype(F32)

            whole = lax.fori_loop(1, n, add, parts[which, mine].astype(F32))
            collected[which, mine] = whole.astype(BF)

            def hand(off, carry):
                all_copy(which, off, mine, lax.rem(v + off, n)).start()
                return carry

            lax.fori_loop(1, n, hand, 0)

    for which in (0, 1):
        mine = chunk_of(which, v)

        def rest(off, carry, which=which, mine=mine):
            t = lax.rem(v + off, n)
            row_copy(which, off).wait_send()
            chunk = chunk_of(which, t)

            @pl.when(chunk < chunks)
            def _():
                sum_copy(which, off, v, t, chunk).wait_send()
                all_copy(which, off, chunk, t).wait_recv()

            @pl.when(mine < chunks)
            def _():
                all_copy(which, off, mine, t).wait_send()

            return carry

        lax.fori_loop(1, n, rest, 0)

    @pl.when(has_left)
    def _():
        to_left.wait_send()

    @pl.when(has_right)
    def _():
        to_right.wait_send()

    @pl.when(last)
    def _():
        guarded(step_copies(seed, 0, s), lambda c: c.wait_send(), False)

    @pl.when(s > 0)
    def _():
        guarded(step_copies(out, 1, s - 1), lambda c: c.wait_send(), True)


def finish(per, scales, grad, collected, grad_out, fine_out, coarse_out):
    channels = fine_out.shape[1]
    grad_out[...] = jnp.swapaxes(grad[...], 0, 1)
    for which, ref in enumerate((fine_out, coarse_out)):
        for k in range(TAPS):
            at = (k % per) * channels
            value = collected[which, k // per, :, at:at + channels]
            ref[k] = value.astype(F32) * scales[which]


def on_device(
    cotangent, labels, class_weight, inputs, fine_pre, pooled, coarse_pre,
    fine_filters, coarse_filters,
):
    segments = lax.axis_size("segment")
    n = lax.axis_size("vol")
    channels, depth, plane = inputs.shape[1:]
    own = depth * plane
    cw = plane // 4
    cdepth = depth // 2
    row_len = pooled.shape[2] * pooled.shape[3]
    per = -(-TAPS // n)
    chunks = -(-TAPS // per)
    cells = own * n
    scales = (1.0 / math.sqrt(cells), 1.0 / math.sqrt(cells // 8))
    sizes = (segments, n, channels, depth, plane, per, chunks)
    chunk_shape = (channels, per * channels)
    vmem = pl.BlockSpec(memory_space=pltpu.VMEM)
    dma = pltpu.SemaphoreType.DMA
    grad, collected = pl.pallas_call(
        functools.partial(kernel, sizes),
        out_shape=(
            jax.ShapeDtypeStruct((depth, channels, plane), BF),
            jax.ShapeDtypeStruct((2, chunks, *chunk_shape), BF),
        ),
        in_specs=[pl.BlockSpec(memory_space=pltpu.SMEM)] + [vmem] * 8,
        out_specs=(vmem, vmem),
        scratch_shapes=[
            pltpu.VMEM((depth, channels, plane), BF),
            pltpu.VMEM((3 * channels, 9 * channels), BF),
            pltpu.VMEM((3 * channels, 9 * channels), BF),
            pltpu.VMEM((n, channels, row_len), BF),
            pltpu.VMEM((n, channels, row_len), BF),
            pltpu.VMEM((depth + 2, channels, plane), BF),
            pltpu.VMEM((depth + 2, channels, plane), BF),
            pltpu.VMEM((3, channels, cdepth * cw), BF),
            pltpu.VMEM((2, channels, cdepth * cw), BF),
            pltpu.VMEM((channels, (cdepth + 4) * cw), BF),
            pltpu.VMEM((3 * channels, own + 2 * plane), BF),
            pltpu.VMEM((3 * channels, (cdepth + 4) * cw), BF),
            pltpu.VMEM((9 * channels, own + 2 * plane), BF),
            pltpu.VMEM((9 * channels, (cdepth + 4) * cw), BF),
            pltpu.VMEM((2, chunks, *chunk_shape), BF),
            pltpu.VMEM((2, n, *chunk_shape), BF),
            dma((2, n)), dma((2, n)), dma((2,)), dma((2,)), dma((2, 6)), dma((6,)),
            dma((2, n)), dma((2, n)), dma((2, n)), dma((2, chunks)),
        ],
        compiler_params=pltpu.CompilerParams(
            collective_id=0, has_side_effects=True, vmem_limit_bytes=60 * 1024 * 1024
        ),
    )(
        class_weight,
        cotangent,
        labels,
        inputs[0],
        fine_pre[0],
        coarse_pre[0].reshape(channels, row_len),
        pooled[0].reshape(channels, row_len),
        fine_filters[0],
        coarse_filters[0],
    )

    tap_shape = jax.ShapeDtypeStruct((TAPS, channels, channels), F32)
    grad, fine_grads, coarse_grads = pl.pallas_call(
        functools.partial(finish, per, scales),
        out_shape=(jax.ShapeDtypeStruct((channels, depth, plane), BF), tap_shape, tap_shape),
        in_specs=[vmem] * 2,
        out_specs=(vmem, vmem, vmem),
    )(grad, collected)
    return (grad[None], fine_grads[None], coarse_grads[None])


def solution(mesh):
    return jax.shard_map(
        on_device,
        mesh=mesh,
        in_specs=(
            P(None, "vol", None),
            P("vol", None),
            P(),
            P("segment", None, "vol", None),
            P("segment", None, "vol", None),
            P("segment", None, "vol", None),
            P("segment", None, "vol", None),
            P("segment", None, None, None),
            P("segment", None, None, None),
        ),
        out_specs=(
            P("segment", None, "vol", None),
            P("segment", None, None, None),
            P("segment", None, None, None),
        ),
        check_vma=False,
    )
```

profile of v0, /device:TPU:0, one launch (start us, length us, event | category | flops | bytes accessed | tf_op | source)
XLA Modules:
  0.0 55.4 jit_solution(2715700117356044433)
XLA Ops:
  0.6 52.1 %shard_map.112 = (bf16[4,64,256]{2,1,0:T(8,128)(2,1)}, bf16[2,7,64,256]{3,2,1,0:T(8,128)(2,1)}) custom-call(f32[3]{0:T(128)} %class_weight.1, bf16[64,4,256]{2,1,0:T(4,128)(2,1)} %cotangent.1, s32[4,256]{1,0:T(4,128)} %labels.1, bf16[64,4,256]{2,1,0:T(4,128)(2,1)} %bitcast.11, bf16[64,4,256]{2,1,0:T(4,128)(2,1)} %bitcast.12, bf16[64,128]{1,0:T(8,128)(2,1)} %bitcast.13, ...), custom_call_target="tpu_custom_call" | custom-call | tf_op jit(solution)/shard_map/pallas_call | solution.py:493
  52.8 2.6 %shard_map.113 = (bf16[64,4,256]{2,1,0:T(4,128)(2,1)}, f32[27,64,64]{2,1,0:T(8,128)}, f32[27,64,64]{2,1,0:T(8,128)}) custom-call(bf16[4,64,256]{2,1,0:T(8,128)(2,1)} %get-tuple-element.8.grad, bf16[2,7,64,256]{3,2,1,0:T(8,128)(2,1)} %get-tuple-element.9.collected), custom_call_target="tpu_custom_call" | custom-call | tf_op jit(solution)/shard_map/pallas_call | solution.py:537
where the time goes:
time: 55.5 us; the launch traced here: 55.4 us
  Pallas kernels  54.7 us (99%)
  between operations  0.64 us (1%)
    pallas_call x1, Pallas kernels, on_device(): pl.pallas_call(functools.partial(kernel, sizes), out_shape=(jax.ShapeDtyp...  52.1 us
    pallas_call x1, Pallas kernels, on_device(): pl.pallas_call(functools.partial(finish, per, scales), out_shape=(jax.Sha...  2.59 us

commit v1 on v0

v1 whole, which is shorter than its diff:
```python
import functools
import math

import jax
import jax.numpy as jnp
from jax import lax
from jax.experimental import pallas as pl
from jax.experimental.pallas import tpu as pltpu
from jax.sharding import PartitionSpec as P

XL = 16
HX = XL // 2
TAPS = 27
OWNERS = 4
GROUP_LANES = 1024
MIB = 1024 * 1024
PICK_BYTES = 4 * MIB
BF = jnp.bfloat16
F32 = jnp.float32


def iota(shape, dim):
    return lax.broadcasted_iota(jnp.int32, shape, dim)


def matmul(a, b):
    return lax.dot_general(a, b, (((1,), (0,)), ((), ())), preferred_element_type=F32)


def matmul_nt(a, b):
    return lax.dot_general(a, b, (((1,), (1,)), ((), ())), preferred_element_type=F32)


def tap_mask(lanes, plane, columns, row_step, col_step):
    lane = iota((1, lanes), 1)
    column = lax.rem(lane, columns) - col_step
    row = lax.div(lax.rem(lane, plane), columns) - row_step
    rows = plane // columns
    inside = (column >= 0) & (column < columns) & (row >= 0) & (row < rows)
    return jnp.where(inside, 1.0, 0.0).astype(BF)


def rolled(value, shift):
    size = value.shape[1]
    shift = shift % size
    return value if shift == 0 else pltpu.roll(value, shift, 1)


STEPS = [(r, c) for r in (-1, 0, 1) for c in (-1, 0, 1)]


def kernel(
    sizes, scales,
    class_weight_h, cotangent_h, labels_h, saved_h, fine_pre_h, coarse_pre_h, pooled_h,
    fine_w_h, coarse_w_h,
    grad_out, fine_out, coarse_out,
    class_weight, cotangent, labels, saved, fine_pre, fine_w, coarse_w,
    out, seed, fine_cat, coarse_cat, pre_rows, pool_rows, pre_ext, x_ext, grad_ext, pool_ext,
    pool_out, coarse_gate, pick, pool_matrix, fine_x, pool_all, fine_cols, coarse_cols,
    full_cols, gz_all, parts, arrived, collected,
    load_sem, row_send, row_recv, halo_send, halo_recv, step_send, step_recv,
    sum_send, sum_recv, all_send, all_recv, gz_send, gz_recv, go,
):
    segments, n, channels, depth, plane = sizes
    cw = plane // 4
    cdepth = depth // 2
    own = depth * plane
    slab = cdepth * cw
    row_len = coarse_pre_h.shape[1]
    groups = pool_all.shape[0]
    group = pool_all.shape[2]
    s = lax.axis_index("segment")
    v = lax.axis_index("vol")
    has_left, has_right = v > 0, v < n - 1
    last = s == segments - 1
    late = s >= segments - 2
    first_owner = n // 2 - OWNERS // 2
    mine = v - first_owner
    owner = (mine >= 0) & (mine < OWNERS)
    share = 3 * channels // OWNERS

    def put(src, dst, send, recv, segment, vol):
        return pltpu.make_async_remote_copy(
            src_ref=src, dst_ref=dst, send_sem=send, recv_sem=recv,
            device_id=(segment, vol), device_id_type=pl.DeviceIdType.MESH,
        )

    def credit(segment):
        pl.semaphore_signal(
            go, inc=1, device_id=(segment, v), device_id_type=pl.DeviceIdType.MESH
        )

    barrier = pltpu.get_barrier_semaphore()

    def greet(off, carry):
        pl.semaphore_signal(
            barrier, inc=1, device_id=(s, lax.rem(v + off, n)),
            device_id_type=pl.DeviceIdType.MESH,
        )
        return carry

    lax.fori_loop(1, n, greet, 0)
    for up in (-1, 1):
        for side in (-1, 0, 1):
            there = (s + up >= 0) & (s + up < segments) & (v + side >= 0) & (v + side < n)

            @pl.when(there)
            def _(up=up, side=side):
                pl.semaphore_signal(
                    barrier, inc=1, device_id=(s + up, v + side),
                    device_id_type=pl.DeviceIdType.MESH,
                )

    def load(src, dst, index):
        return pltpu.make_async_copy(src, dst, load_sem.at[index])

    rows_load = load(coarse_pre_h, pre_rows.at[v], 0)
    pre_load = load(fine_pre_h, fine_pre, 1)
    seed_loads = (
        load(class_weight_h, class_weight, 2),
        load(cotangent_h, cotangent, 3),
        load(labels_h, labels, 4),
    )
    coarse_w_load = load(coarse_w_h, coarse_w, 5)
    fine_w_load = load(fine_w_h, fine_w, 6)
    saved_load = load(saved_h, saved, 7)
    pooled_load = load(pooled_h, pool_rows.at[v], 8)

    rows_load.start()

    @pl.when(last)
    def _():
        for copy in seed_loads:
            copy.start()

    for copy in (pre_load, coarse_w_load, fine_w_load, saved_load, pooled_load):
        copy.start()

    fine_lane = iota((1, own), 1)
    pool_target = (
        lax.div(fine_lane, 2 * plane) * cw
        + lax.div(lax.rem(fine_lane, plane), 2 * XL) * HX
        + lax.div(lax.rem(fine_lane, XL), 2)
    )
    pool_matrix[...] = jnp.where(iota((slab, own), 0) == pool_target, 1.0, 0.0).astype(BF)

    up_lane = iota((1, plane), 1)
    up_target = lax.div(up_lane, 2 * XL) * HX + lax.div(lax.rem(up_lane, XL), 2)
    up_matrix = jnp.where(iota((cw, plane), 0) == up_target, 0.125, 0.0).astype(BF)

    reach = cdepth + 4
    reach_lane = iota((1, reach * cw), 1)
    reach_depth = v * cdepth - 2 + lax.div(reach_lane, cw)
    reach_cell = reach_depth * HX + lax.rem(reach_lane, HX)
    reach_cell = jnp.where(
        (reach_depth >= 0) & (reach_depth < n * cdepth), reach_cell, -1
    )
    reach_inline = lax.div(lax.rem(reach_lane, cw), HX)
    whole_pick = pick.shape[0] > 1

    def picked(rows, u, cell, inline, lanes):
        chosen = iota((row_len, lanes), 0) == jnp.where(inline == u, cell, -1)
        return matmul(rows[u], jnp.where(chosen, 1.0, 0.0).astype(BF))

    if whole_pick:
        for u in range(n):
            chosen = iota((row_len, reach * cw), 0) == jnp.where(reach_inline == u, reach_cell, -1)
            pick[u * row_len:(u + 1) * row_len, :] = jnp.where(chosen, 1.0, 0.0).astype(BF)

    def step_copies(src, turn, segment):
        def step(which, a, b, vol):
            return put(a, b, step_send.at[turn, which], step_recv.at[which], segment, vol)

        block = pool_out.at[turn]
        planes = [step(5 + p, src.at[p], grad_ext.at[p + 1], v) for p in range(depth)]
        return (
            step(0, block, pool_ext.at[1], v),
            step(1, block, pool_ext.at[2], v - 1),
            step(2, block, pool_ext.at[0], v + 1),
            step(3, src.at[0], grad_ext.at[depth + 1], v - 1),
            step(4, src.at[depth - 1], grad_ext.at[0], v + 1),
            *planes,
        )

    def on_left(act, *copies):
        @pl.when(has_left)
        def _():
            for copy in copies:
                act(copy)

    def on_right(act, *copies):
        @pl.when(has_right)
        def _():
            for copy in copies:
                act(copy)

    def start(copy):
        copy.start()

    def wait_send(copy):
        copy.wait_send()

    def wait_recv(copy):
        copy.wait_recv()

    def pool_of(ref):
        flat = jnp.concatenate([ref[p] for p in range(depth)], axis=1)
        return matmul_nt(flat, pool_matrix[...]).astype(BF)

    @pl.when(last)
    def _():
        for copy in seed_loads:
            copy.wait()
        planes = jnp.swapaxes(cotangent[...], 0, 1)
        for p in range(depth):
            label = labels[p:p + 1, :]
            weight = jnp.zeros(label.shape, F32)
            for index in range(class_weight.shape[0]):
                weight = weight + jnp.where(label == index, class_weight[index], 0.0)
            block = (planes[p].astype(F32) * weight).astype(BF)
            seed[p] = block
            grad_ext[p + 1] = block
        pool_out[0] = pool_of(seed)
        pool_ext[1] = pool_out[0]

    pre_load.wait()
    pre_ext[1:depth + 1] = jnp.swapaxes(fine_pre[...], 0, 1)
    coarse_w_load.wait()
    fine_w_load.wait()
    for k in range(TAPS):
        rows = slice(k // 9 * channels, (k // 9 + 1) * channels)
        lanes = slice(k % 9 * channels, (k % 9 + 1) * channels)
        coarse_cat[rows, lanes] = coarse_w[k]
        fine_cat[rows, lanes] = fine_w[k]
    saved_load.wait()
    x_ext[1:depth + 1] = jnp.swapaxes(saved[...], 0, 1)

    @pl.when(v == 0)
    def _():
        pre_ext[0] = jnp.zeros((channels, plane), BF)
        x_ext[0] = jnp.zeros((channels, plane), BF)
        grad_ext[0] = jnp.zeros((channels, plane), BF)
        pool_ext[0] = jnp.zeros(pool_ext.shape[1:], BF)

    @pl.when(v == n - 1)
    def _():
        pre_ext[depth + 1] = jnp.zeros((channels, plane), BF)
        x_ext[depth + 1] = jnp.zeros((channels, plane), BF)
        grad_ext[depth + 1] = jnp.zeros((channels, plane), BF)
        pool_ext[2] = jnp.zeros(pool_ext.shape[1:], BF)

    rows_load.wait()
    pooled_load.wait()

    ups = jnp.where(s > 0, 1, 0) + jnp.where(last, 0, 1)
    sides = 1 + jnp.where(has_left, 1, 0) + jnp.where(has_right, 1, 0)
    pl.semaphore_wait(barrier, n - 1 + ups * sides)

    def halo(ref, index):
        return (
            put(ref.at[1], ref.at[depth + 1], halo_send.at[index], halo_recv.at[index], s, v - 1),
            put(
                ref.at[depth], ref.at[0],
                halo_send.at[index + 1], halo_recv.at[index + 1], s, v + 1,
            ),
        )

    pre_left, pre_right = halo(pre_ext, 0)
    x_left, x_right = halo(x_ext, 2)

    def row_copy(which, off):
        ref = (pre_rows, pool_rows, gz_all)[which]
        return put(
            ref.at[v], ref.at[v], row_send.at[which, off], row_recv.at[which, v],
            s, lax.rem(v + off, n),
        )

    def send_rows(which):
        def body(off, carry):
            row_copy(which, off).start()
            return carry

        lax.fori_loop(1, n, body, 0)

    def wait_rows(which):
        ref = (pre_rows, pool_rows, gz_all)[which]

        def body(off, carry):
            u = lax.rem(v + off, n)
            put(
                ref.at[u], ref.at[u], row_send.at[which, off], row_recv.at[which, u], s, u
            ).wait_recv()
            return carry

        lax.fori_loop(1, n, body, 0)

    @pl.when(last)
    def _():
        send_rows(0)
        copies = step_copies(seed, 0, s)
        on_left(start, copies[1], copies[3], pre_left)
        on_right(start, copies[2], copies[4], pre_right)

    @pl.when(jnp.logical_not(last))
    def _():
        @pl.when(s == segments - 2)
        def _():
            pl.semaphore_wait(go, 1)

        send_rows(0)
        on_left(start, pre_left, x_left)
        on_right(start, pre_right, x_right)

    wait_rows(0)

    @pl.when(last)
    def _():
        credit(s - 1)

    if whole_pick:
        flat_rows = jnp.concatenate([pre_rows[u] for u in range(n)], axis=1)
        coarse_gate[...] = matmul(flat_rows, pick[...]).astype(BF)
    else:
        coarse_gate[...] = lax.fori_loop(
            0, n,
            lambda u, total: total + picked(
                pre_rows, u, reach_cell, reach_inline, reach * cw
            ),
            jnp.zeros((channels, reach * cw), F32),
        ).astype(BF)

    def take_pooled():
        wait_rows(1)
        lane = iota((1, group), 1)
        inline = lax.div(lax.rem(lane, cw), HX)

        def body(g, carry):
            cell = (g * (group // cw) + lax.div(lane, cw)) * HX + lax.rem(lane, HX)
            pool_all[g] = lax.fori_loop(
                0, n,
                lambda u, total: total + picked(pool_rows, u, cell, inline, group),
                jnp.zeros((channels, group), F32),
            ).astype(BF)
            return carry

        lax.fori_loop(0, groups, body, 0)

    def take_fine_x():
        for outer in range(3):
            for p in range(depth):
                fine_x[outer * channels:(outer + 1) * channels, p * plane:(p + 1) * plane] = (
                    x_ext[p + outer]
                )

    @pl.when(jnp.logical_not(late))
    def _():
        send_rows(1)
        take_pooled()

    @pl.when(jnp.logical_not(last))
    def _():
        on_left(wait_recv, pre_right, x_right)
        on_right(wait_recv, pre_left, x_left)
        take_fine_x()

    incoming = step_copies(out, 1, s)

    @pl.when(jnp.logical_not(last))
    def _():
        incoming[0].wait_recv()

    on_left(wait_recv, incoming[2])
    on_right(wait_recv, incoming[1])

    side = pool_ext.shape[2]
    near = jnp.concatenate(
        [pool_ext[0][:, side - 2 * cw:], pool_ext[1], pool_ext[2][:, :2 * cw]], axis=1
    )
    coarse_gz = jnp.where(coarse_gate[...] > 0, near, jnp.zeros_like(near))
    gz_all[v] = coarse_gz[:, 2 * cw:2 * cw + slab]
    for r, (row_step, col_step) in enumerate(STEPS):
        mask = tap_mask(reach * cw, cw, HX, row_step, col_step)
        coarse_cols[r * channels:(r + 1) * channels, :] = (
            rolled(coarse_gz, row_step * HX + col_step) * mask
        )

    @pl.when(s == 0)
    def _():
        send_rows(2)

    terms = matmul(coarse_cat[...], coarse_cols[...])
    width = (cdepth + 2) * cw
    coarse_back = sum(
        terms[outer * channels:(outer + 1) * channels, (2 - outer) * cw:(2 - outer) * cw + width]
        for outer in range(3)
    ).astype(BF)

    pieces = []
    for p in range(depth + 2):
        j = (p + 1) // 2
        if p and j == p // 2:
            spread = pieces[-1]
        else:
            spread = matmul(coarse_back[:, j * cw:(j + 1) * cw], up_matrix)
        pieces.append(spread)

    @pl.when(last)
    def _():
        on_left(wait_recv, pre_right)
        on_right(wait_recv, pre_left)

    masks = [tap_mask(plane, plane, XL, *step) for step in STEPS]
    for p in (1, 0, depth + 1, *range(2, depth + 1)):
        if p == 0:
            on_left(wait_recv, incoming[4])
        elif p == depth + 1:
            on_right(wait_recv, incoming[3])
        else:
            @pl.when(jnp.logical_not(last))
            def _(p=p):
                incoming[4 + p].wait_recv()

        grad = grad_ext[p].astype(F32) + pieces[p]
        gz = jnp.where(pre_ext[p].astype(F32) > 0, grad, 0.0).astype(BF)
        for r, (row_step, col_step) in enumerate(STEPS):
            fine_cols[r * channels:(r + 1) * channels, p * plane:(p + 1) * plane] = (
                rolled(gz, row_step * XL + col_step) * masks[r]
            )

    @pl.when(s == segments - 2)
    def _():
        credit(s + 1)

    def sum_copy(j, vol_from, vol_to):
        return put(
            parts.at[j], arrived.at[vol_from],
            sum_send.at[j], sum_recv.at[vol_from], s, vol_to,
        )

    def fine_sums():
        grads = matmul_nt(fine_x[...], fine_cols[:, plane:plane + own]).astype(BF)
        for j in range(OWNERS):
            parts[j] = grads[j * share:(j + 1) * share, :]
        for j in range(OWNERS):
            @pl.when(v != first_owner + j)
            def _(j=j):
                sum_copy(j, v, first_owner + j).start()

            @pl.when(v == first_owner + j)
            def _(j=j):
                arrived[v] = parts[j]

    @pl.when(s == 0)
    def _():
        fine_sums()

    outgoing = step_copies(out, 1, s - 1)
    terms = matmul(fine_cat[...], fine_cols[...])
    for p in range(depth):
        total = grad_ext[p + 1].astype(F32)
        for outer in range(3):
            total = total + terms[
                outer * channels:(outer + 1) * channels,
                (p + 2 - outer) * plane:(p + 3 - outer) * plane,
            ]
        out[p] = total.astype(BF)

    @pl.when(s > 0)
    def _():
        outgoing[5].start()
        pool_out[1] = pool_of(out)
        on_left(start, outgoing[1])
        on_right(start, outgoing[2])
        outgoing[0].start()
        on_left(start, outgoing[3])
        on_right(start, outgoing[4])
        for p in range(1, depth):
            outgoing[5 + p].start()

    @pl.when(last)
    def _():
        pl.semaphore_wait(go, 1)
        on_left(start, x_left)
        on_right(start, x_right)

    @pl.when(late)
    def _():
        send_rows(1)
        take_pooled()

    @pl.when(last)
    def _():
        on_left(wait_recv, x_right)
        on_right(wait_recv, x_left)
        take_fine_x()

    @pl.when(s > 0)
    def _():
        fine_sums()
        send_rows(2)

    grad_out[...] = jnp.swapaxes(out[...], 0, 1)

    def coarse_sums():
        total = jnp.zeros((3 * channels, 9 * channels), F32)
        edge = jnp.zeros((channels, cw), BF)
        for g in range(groups):
            xs = jnp.concatenate(
                [
                    pool_all[g - 1][:, group - cw:] if g else edge,
                    pool_all[g],
                    pool_all[g + 1][:, :cw] if g < groups - 1 else edge,
                ],
                axis=1,
            )
            tall = jnp.concatenate([xs[:, o * cw:o * cw + group] for o in range(3)], axis=0)
            slabs = group // slab
            flat = jnp.concatenate([gz_all[g * slabs + u] for u in range(slabs)], axis=1)
            for r, (row_step, col_step) in enumerate(STEPS):
                mask = tap_mask(group, cw, HX, row_step, col_step)
                full_cols[r * channels:(r + 1) * channels, :] = (
                    rolled(flat, row_step * HX + col_step) * mask
                )
            total = total + matmul_nt(tall, full_cols[...])
        return total * scales[1]

    def place(ref, first_row, value):
        rows = value.shape[0]
        at = first_row
        while at < first_row + rows:
            outer, inner = divmod(at, channels)
            count = min(channels - inner, first_row + rows - at)
            for r in range(9):
                ref[outer * 9 + r, inner:inner + count, :] = value[
                    at - first_row:at - first_row + count, r * channels:(r + 1) * channels
                ]
            at += count

    def all_copy(j, off, vol_to):
        return put(
            collected.at[j], collected.at[j], all_send.at[off], all_recv.at[j], s, vol_to
        )

    @pl.when(owner)
    def _():
        def arrive(off, carry):
            u = lax.rem(v + off, n)
            sum_copy(0, u, u).wait_recv()
            return carry

        lax.fori_loop(1, n, arrive, 0)
        whole = arrived[0].astype(F32)
        for u in range(1, n):
            whole = whole + arrived[u].astype(F32)
        collected[mine] = whole.astype(BF)

        def hand(off, carry):
            all_copy(mine, off, lax.rem(v + off, n)).start()
            return carry

        lax.fori_loop(1, n, hand, 0)

    wait_rows(2)
    place(coarse_out, 0, coarse_sums())

    for j in range(OWNERS):
        @pl.when(v != first_owner + j)
        def _(j=j):
            all_copy(j, 0, v).wait_recv()

        place(fine_out, j * share, collected[j].astype(F32) * scales[0])

    def rest(off, carry):
        for which in range(3):
            row_copy(which, off).wait_send()

        @pl.when(owner)
        def _():
            all_copy(mine, off, lax.rem(v + off, n)).wait_send()

        return carry

    lax.fori_loop(1, n, rest, 0)
    for j in range(OWNERS):
        @pl.when(v != first_owner + j)
        def _(j=j):
            sum_copy(j, v, first_owner + j).wait_send()

    on_left(wait_send, pre_left, x_left)
    on_right(wait_send, pre_right, x_right)

    @pl.when(last)
    def _():
        copies = step_copies(seed, 0, s)
        on_left(wait_send, copies[1], copies[3])
        on_right(wait_send, copies[2], copies[4])

    @pl.when(s > 0)
    def _():
        on_left(wait_send, outgoing[1], outgoing[3])
        on_right(wait_send, outgoing[2], outgoing[4])
        wait_send(outgoing[0])
        for p in range(depth):
            wait_send(outgoing[5 + p])


def finish(grad, fine, coarse, grad_out, fine_out, coarse_out, sem):
    copies = [
        pltpu.make_async_copy(src, dst, sem.at[index])
        for index, (src, dst) in enumerate(
            ((fine, fine_out), (coarse, coarse_out), (grad, grad_out))
        )
    ]
    for copy in copies:
        copy.start()
    for copy in copies:
        copy.wait()


def on_device(
    cotangent, labels, class_weight, inputs, fine_pre, pooled, coarse_pre,
    fine_filters, coarse_filters,
):
    segments = lax.axis_size("segment")
    n = lax.axis_size("vol")
    channels, depth, plane = inputs.shape[1:]
    own = depth * plane
    cw = plane // 4
    cdepth = depth // 2
    slab = cdepth * cw
    reach = cdepth + 4
    row_len = pooled.shape[2] * pooled.shape[3]
    cells = own * n
    scales = (1.0 / math.sqrt(cells), 1.0 / math.sqrt(cells // 8))
    sizes = (segments, n, channels, depth, plane)
    group = min(GROUP_LANES, n * slab)
    groups = n * slab // group
    share = 3 * channels // OWNERS
    pick_shape = (n * row_len, reach * cw)
    if math.prod(pick_shape) * 2 > PICK_BYTES:
        pick_shape = (1, 128)
    vmem = pl.BlockSpec(memory_space=pltpu.VMEM)
    limit = min(60 * MIB, 16 * MIB + 6 * 2 * 9 * channels * (own + 2 * plane))
    hbm = pl.BlockSpec(memory_space=pltpu.HBM)
    dma = pltpu.SemaphoreType.DMA
    tap_shape = jax.ShapeDtypeStruct((TAPS, channels, channels), F32)
    grad_shape = jax.ShapeDtypeStruct((channels, depth, plane), BF)
    outs = pl.pallas_call(
        functools.partial(kernel, sizes, scales),
        out_shape=(grad_shape, tap_shape, tap_shape),
        in_specs=[hbm] * 9,
        out_specs=(vmem, vmem, vmem),
        scratch_shapes=[
            pltpu.SMEM(class_weight.shape, F32),
            pltpu.VMEM(cotangent.shape, BF),
            pltpu.VMEM(labels.shape, jnp.int32),
            pltpu.VMEM((channels, depth, plane), BF),
            pltpu.VMEM((channels, depth, plane), BF),
            pltpu.VMEM((TAPS, channels, channels), BF),
            pltpu.VMEM((TAPS, channels, channels), BF),
            pltpu.VMEM((depth, channels, plane), BF),
            pltpu.VMEM((depth, channels, plane), BF),
            pltpu.VMEM((3 * channels, 9 * channels), BF),
            pltpu.VMEM((3 * channels, 9 * channels), BF),
            pltpu.VMEM((n, channels, row_len), BF),
            pltpu.VMEM((n, channels, row_len), BF),
            pltpu.VMEM((depth + 2, channels, plane), BF),
            pltpu.VMEM((depth + 2, channels, plane), BF),
            pltpu.VMEM((depth + 2, channels, plane), BF),
            pltpu.VMEM((3, channels, slab), BF),
            pltpu.VMEM((2, channels, slab), BF),
            pltpu.VMEM((channels, reach * cw), BF),
            pltpu.VMEM(pick_shape, BF),
            pltpu.VMEM((slab, own), BF),
            pltpu.VMEM((3 * channels, own), BF),
            pltpu.VMEM((groups, channels, group), BF),
            pltpu.VMEM((9 * channels, own + 2 * plane), BF),
            pltpu.VMEM((9 * channels, reach * cw), BF),
            pltpu.VMEM((9 * channels, group), BF),
            pltpu.VMEM((n, channels, slab), BF),
            pltpu.VMEM((OWNERS, share, 9 * channels), BF),
            pltpu.VMEM((n, share, 9 * channels), BF),
            pltpu.VMEM((OWNERS, share, 9 * channels), BF),
            dma((9,)), dma((3, n)), dma((3, n)), dma((4,)), dma((4,)),
            dma((2, 5 + depth)), dma((5 + depth,)),
            dma((OWNERS,)), dma((n,)), dma((n,)), dma((OWNERS,)), dma((1,)), dma((1,)),
            pltpu.SemaphoreType.REGULAR,
        ],
        compiler_params=pltpu.CompilerParams(
            collective_id=0, has_side_effects=True, vmem_limit_bytes=limit
        ),
    )(
        *(
            pltpu.with_memory_space_constraint(array, pltpu.HBM)
            for array in (
                class_weight,
                cotangent,
                labels,
                inputs[0],
                fine_pre[0],
                coarse_pre[0].reshape(channels, row_len),
                pooled[0].reshape(channels, row_len),
                fine_filters[0],
                coarse_filters[0],
            )
        )
    )

    spaces = pl.BlockSpec(memory_space=pl.ANY)
    grad, fine_grads, coarse_grads = pl.pallas_call(
        finish,
        out_shape=(grad_shape, tap_shape, tap_shape),
        in_specs=[spaces] * 3,
        out_specs=[hbm] * 3,
        scratch_shapes=[dma((3,))],
        compiler_params=pltpu.CompilerParams(vmem_limit_bytes=1024 * 1024),
    )(*outs)
    return (grad[None], fine_grads[None], coarse_grads[None])


def solution(mesh):
    return jax.shard_map(
        on_device,
        mesh=mesh,
        in_specs=(
            P(None, "vol", None),
            P("vol", None),
            P(),
            P("segment", None, "vol", None),
            P("segment", None, "vol", None),
            P("segment", None, "vol", None),
            P("segment", None, "vol", None),
            P("segment", None, None, None),
            P("segment", None, None, None),
        ),
        out_specs=(
            P("segment", None, "vol", None),
            P("segment", None, None, None),
            P("segment", None, None, None),
        ),
        check_vma=False,
    )
```

time: 55.5 us -> 44.7 us (0.81)
  Pallas kernels: 54.7 us -> 43.9 us
    pallas_call x2, Pallas kernels: 54.7 us -> 43.9 us  [the longest x1 42.7 us: on_device(): pl.pallas_call(functools.partial(kernel, sizes, scales), out_shape=(grad_...]
where the time goes in v1:
time: 44.7 us; the launch traced here: 44.6 us
  Pallas kernels  43.9 us (98%)
  between operations  0.64 us (1%)
    pallas_call x1, Pallas kernels, on_device(): pl.pallas_call(functools.partial(kernel, sizes, scales), out_shape=(grad_...  42.7 us
    pallas_call x1, Pallas kernels, on_device(): pl.pallas_call(finish, out_shape=(grad_shape, tap_shape, tap_shape), in_s...  1.27 us

profile of v1, /device:TPU:0, one launch (start us, length us, event | category | flops | bytes accessed | tf_op | source)
XLA Modules:
  0.0 44.6 jit_solution(98741688971280436)
XLA Ops:
  0.6 42.7 %shard_map.112 = (bf16[64,4,256]{2,1,0:T(4,128)(2,1)S(1)}, f32[27,64,64]{2,1,0:T(8,128)S(1)}, f32[27,64,64]{2,1,0:T(8,128)S(1)}) custom-call(f32[3]{0:T(128)} %class_weight_h.1, bf16[64,4,256]{2,1,0:T(4,128)(2,1)} %cotangent_h.1, s32[4,256]{1,0:T(4,128)} %labels_h.1, bf16[64,4,256]{2,1,0:T(4,128)(2,1)} %bitcast.11, bf16[64,4,256]{2,1,0:T(4,128)(2,1)} %bitcast.12, ...), custom_call_target="tpu_custom_call" | custom-call | tf_op jit(solution)/shard_map/pallas_call | solution.py:648
  43.3 1.3 %shard_map.113 = (bf16[64,4,256]{2,1,0:T(4,128)(2,1)}, f32[27,64,64]{2,1,0:T(8,128)}, f32[27,64,64]{2,1,0:T(8,128)}) custom-call(bf16[64,4,256]{2,1,0:T(4,128)(2,1)S(1)} %get-tuple-element.9.grad, f32[27,64,64]{2,1,0:T(8,128)S(1)} %get-tuple-element.10.fine, f32[27,64,64]{2,1,0:T(8,128)S(1)} %get-tuple-element.11.coarse), custom_call_target="tpu_custom_call" | custom-call | tf_op jit(solution)/shard_map/pallas_call | solution.py:710

commit v2 on v1

--- a/solution.py
+++ b/solution.py
@@ -11,7 +11,8 @@
 XL = 16
 HX = XL // 2
 TAPS = 27
-OWNERS = 4
+KEEPERS = 4
+PARTS = 3
 GROUP_LANES = 1024
 MIB = 1024 * 1024
 PICK_BYTES = 4 * MIB
@@ -53,13 +54,14 @@
     sizes, scales,
     class_weight_h, cotangent_h, labels_h, saved_h, fine_pre_h, coarse_pre_h, pooled_h,
     fine_w_h, coarse_w_h,
-    grad_out, fine_out, coarse_out,
-    class_weight, cotangent, labels, saved, fine_pre, fine_w, coarse_w,
+    grad_o, fine_o, coarse_o,
+    grad_out, fine_out, coarse_out, class_weight, cotangent, labels, saved, fine_pre, weights,
     out, seed, fine_cat, coarse_cat, pre_rows, pool_rows, pre_ext, x_ext, grad_ext, pool_ext,
     pool_out, coarse_gate, pick, pool_matrix, fine_x, pool_all, fine_cols, coarse_cols,
-    full_cols, gz_all, parts, arrived, collected,
+    full_cols, gz_all, parts, landed, paired, middle, arrived, collected,
     load_sem, row_send, row_recv, halo_send, halo_recv, step_send, step_recv,
-    sum_send, sum_recv, all_send, all_recv, gz_send, gz_recv, go,
+    pair_send, pair_recv, sum_send, sum_recv, hand_send, pass_send, all_recv,
+    straight_send, straight_recv, spread_send, store_sem, go,
 ):
     segments, n, channels, depth, plane = sizes
     cw = plane // 4
@@ -74,10 +76,19 @@
     has_left, has_right = v > 0, v < n - 1
     last = s == segments - 1
     late = s >= segments - 2
-    first_owner = n // 2 - OWNERS // 2
-    mine = v - first_owner
-    owner = (mine >= 0) & (mine < OWNERS)
-    share = 3 * channels // OWNERS
+    paced = lax.rem(s, 2) == 1
+    direct = jnp.logical_not(paced)
+    half = lax.rem(v, 2)
+    other = 1 - half
+    partner = v + 1 - 2 * half
+    row = lax.div(v, 2)
+    columns = n // 2
+    first_owner = columns // 2 - 1
+    share = 3 * channels // KEEPERS
+    rows_each = share // PARTS
+    first_keeper = n // 2 - KEEPERS // 2
+    mine = v - first_keeper
+    keeper = (mine >= 0) & (mine < KEEPERS)
 
     def put(src, dst, send, recv, segment, vol):
         return pltpu.make_async_remote_copy(
@@ -121,10 +132,11 @@
         load(cotangent_h, cotangent, 3),
         load(labels_h, labels, 4),
     )
-    coarse_w_load = load(coarse_w_h, coarse_w, 5)
-    fine_w_load = load(fine_w_h, fine_w, 6)
-    saved_load = load(saved_h, saved, 7)
-    pooled_load = load(pooled_h, pool_rows.at[v], 8)
+    coarse_w_load = load(coarse_w_h, weights.at[0], 5)
+    fine_w_load = load(fine_w_h, weights.at[1], 5)
+    both_w_load = load(weights, weights, 5)
+    saved_load = load(saved_h, saved, 6)
+    pooled_load = load(pooled_h, pool_rows.at[v], 7)
 
     rows_load.start()
 
@@ -136,13 +148,13 @@
     for copy in (pre_load, coarse_w_load, fine_w_load, saved_load, pooled_load):
         copy.start()
 
-    fine_lane = iota((1, own), 1)
+    fine_lane = iota((own, 1), 0)
     pool_target = (
         lax.div(fine_lane, 2 * plane) * cw
         + lax.div(lax.rem(fine_lane, plane), 2 * XL) * HX
         + lax.div(lax.rem(fine_lane, XL), 2)
     )
-    pool_matrix[...] = jnp.where(iota((slab, own), 0) == pool_target, 1.0, 0.0).astype(BF)
+    pool_matrix[...] = jnp.where(iota((own, slab), 1) == pool_target, 1.0, 0.0).astype(BF)
 
     up_lane = iota((1, plane), 1)
     up_target = lax.div(up_lane, 2 * XL) * HX + lax.div(lax.rem(up_lane, XL), 2)
@@ -169,17 +181,18 @@
 
     def step_copies(src, turn, segment):
         def step(which, a, b, vol):
-            return put(a, b, step_send.at[turn, which], step_recv.at[which], segment, vol)
+            return put(a, b, step_send.at[which], step_recv.at[which], segment, vol)
 
         block = pool_out.at[turn]
-        planes = [step(5 + p, src.at[p], grad_ext.at[p + 1], v) for p in range(depth)]
         return (
             step(0, block, pool_ext.at[1], v),
             step(1, block, pool_ext.at[2], v - 1),
             step(2, block, pool_ext.at[0], v + 1),
             step(3, src.at[0], grad_ext.at[depth + 1], v - 1),
             step(4, src.at[depth - 1], grad_ext.at[0], v + 1),
-            *planes,
+            step(5, src, grad_ext.at[1:depth + 1], v),
+            step(5, src.at[0], grad_ext.at[1], v),
+            step(5, src.at[1:depth], grad_ext.at[2:depth + 1], v),
         )
 
     def on_left(act, *copies):
@@ -205,7 +218,7 @@
 
     def pool_of(ref):
         flat = jnp.concatenate([ref[p] for p in range(depth)], axis=1)
-        return matmul_nt(flat, pool_matrix[...]).astype(BF)
+        return matmul(flat, pool_matrix[...]).astype(BF)
 
     @pl.when(last)
     def _():
@@ -225,13 +238,12 @@
 
     pre_load.wait()
     pre_ext[1:depth + 1] = jnp.swapaxes(fine_pre[...], 0, 1)
-    coarse_w_load.wait()
-    fine_w_load.wait()
+    both_w_load.wait()
     for k in range(TAPS):
         rows = slice(k // 9 * channels, (k // 9 + 1) * channels)
         lanes = slice(k % 9 * channels, (k % 9 + 1) * channels)
-        coarse_cat[rows, lanes] = coarse_w[k]
-        fine_cat[rows, lanes] = fine_w[k]
+        coarse_cat[rows, lanes] = weights[0, k]
+        fine_cat[rows, lanes] = weights[1, k]
     saved_load.wait()
     x_ext[1:depth + 1] = jnp.swapaxes(saved[...], 0, 1)
 
@@ -268,38 +280,52 @@
     pre_left, pre_right = halo(pre_ext, 0)
     x_left, x_right = halo(x_ext, 2)
 
-    def row_copy(which, off):
+    def far_first(act):
+        def body(step, carry):
+            for u in (v + n - step, v - n + step):
+                @pl.when((u >= 0) & (u < n))
+                def _(u=u):
+                    act(u)
+
+            return carry
+
+        lax.fori_loop(1, n, body, 0)
+
+    def others(act):
+        def body(off, carry):
+            act(lax.rem(v + off, n))
+            return carry
+
+        lax.fori_loop(1, n, body, 0)
+
+    def row_copy(which, source, target):
         ref = (pre_rows, pool_rows, gz_all)[which]
         return put(
-            ref.at[v], ref.at[v], row_send.at[which, off], row_recv.at[which, v],
-            s, lax.rem(v + off, n),
-        )
+            ref.at[source], ref.at[source], row_send.at[which], row_recv.at[which], s, target
+        )
+
+    def all_rows(which):
+        ref = (pre_rows, pool_rows, gz_all)[which].at[pl.ds(0, n - 1)]
+        return put(ref, ref, row_send.at[which], row_recv.at[which], s, partner)
 
     def send_rows(which):
-        def body(off, carry):
-            row_copy(which, off).start()
-            return carry
-
-        lax.fori_loop(1, n, body, 0)
+        far_first(lambda u: row_copy(which, v, u).start())
+
+    def send_gz():
+        for off in range(1, n):
+            row_copy(2, v, lax.rem(v + off, n)).start()
 
     def wait_rows(which):
-        ref = (pre_rows, pool_rows, gz_all)[which]
-
-        def body(off, carry):
-            u = lax.rem(v + off, n)
-            put(
-                ref.at[u], ref.at[u], row_send.at[which, off], row_recv.at[which, u], s, u
-            ).wait_recv()
-            return carry
-
-        lax.fori_loop(1, n, body, 0)
+        all_rows(which).wait_recv()
 
     @pl.when(last)
     def _():
+        copies = step_copies(seed, 0, s)
+        on_left(start, copies[1])
+        on_right(start, copies[2])
         send_rows(0)
-        copies = step_copies(seed, 0, s)
-        on_left(start, copies[1], copies[3], pre_left)
-        on_right(start, copies[2], copies[4], pre_right)
+        on_left(start, copies[3], pre_left)
+        on_right(start, copies[4], pre_right)
 
     @pl.when(jnp.logical_not(last))
     def _():
@@ -308,8 +334,13 @@
             pl.semaphore_wait(go, 1)
 
         send_rows(0)
-        on_left(start, pre_left, x_left)
-        on_right(start, pre_right, x_right)
+        on_left(start, pre_left)
+        on_right(start, pre_right)
+
+    @pl.when(jnp.logical_not(late))
+    def _():
+        on_left(start, x_left)
+        on_right(start, x_right)
 
     wait_rows(0)
 
@@ -357,20 +388,20 @@
         send_rows(1)
         take_pooled()
 
-    @pl.when(jnp.logical_not(last))
-    def _():
-        on_left(wait_recv, pre_right, x_right)
-        on_right(wait_recv, pre_left, x_left)
+    @pl.when(jnp.logical_not(late))
+    def _():
+        on_left(wait_recv, x_right)
+        on_right(wait_recv, x_left)
         take_fine_x()
 
     incoming = step_copies(out, 1, s)
-
-    @pl.when(jnp.logical_not(last))
-    def _():
-        incoming[0].wait_recv()
 
     on_left(wait_recv, incoming[2])
     on_right(wait_recv, incoming[1])
+
+    @pl.when(jnp.logical_not(last))
+    def _():
+        incoming[0].wait_recv()
 
     side = pool_ext.shape[2]
     near = jnp.concatenate(
@@ -384,10 +415,6 @@
             rolled(coarse_gz, row_step * HX + col_step) * mask
         )
 
-    @pl.when(s == 0)
-    def _():
-        send_rows(2)
-
     terms = matmul(coarse_cat[...], coarse_cols[...])
     width = (cdepth + 2) * cw
     coarse_back = sum(
@@ -404,55 +431,107 @@
             spread = matmul(coarse_back[:, j * cw:(j + 1) * cw], up_matrix)
         pieces.append(spread)
 
-    @pl.when(last)
-    def _():
-        on_left(wait_recv, pre_right)
-        on_right(wait_recv, pre_left)
-
-    masks = [tap_mask(plane, plane, XL, *step) for step in STEPS]
-    for p in (1, 0, depth + 1, *range(2, depth + 1)):
-        if p == 0:
-            on_left(wait_recv, incoming[4])
-        elif p == depth + 1:
-            on_right(wait_recv, incoming[3])
-        else:
-            @pl.when(jnp.logical_not(last))
-            def _(p=p):
-                incoming[4 + p].wait_recv()
-
+    on_left(wait_recv, pre_right, incoming[4])
+    on_right(wait_recv, pre_left, incoming[3])
+
+    @pl.when(jnp.logical_not(last))
+    def _():
+        incoming[5].wait_recv()
+
+    @pl.when(jnp.logical_not(late) & (s > 0))
+    def _():
+        send_gz()
+
+    gz = []
+    for p in range(depth + 2):
         grad = grad_ext[p].astype(F32) + pieces[p]
-        gz = jnp.where(pre_ext[p].astype(F32) > 0, grad, 0.0).astype(BF)
-        for r, (row_step, col_step) in enumerate(STEPS):
+        gz.append(jnp.where(pre_ext[p].astype(F32) > 0, grad, 0.0).astype(BF))
+    for r, (row_step, col_step) in enumerate(STEPS):
+        mask = tap_mask(plane, plane, XL, row_step, col_step)
+        for p in range(depth + 2):
             fine_cols[r * channels:(r + 1) * channels, p * plane:(p + 1) * plane] = (
-                rolled(gz, row_step * XL + col_step) * masks[r]
+                rolled(gz[p], row_step * XL + col_step) * mask
             )
 
-    @pl.when(s == segments - 2)
-    def _():
-        credit(s + 1)
-
-    def sum_copy(j, vol_from, vol_to):
+    def pair_copy(k):
         return put(
-            parts.at[j], arrived.at[vol_from],
-            sum_send.at[j], sum_recv.at[vol_from], s, vol_to,
+            parts.at[2 * other + k], paired.at[k], pair_send.at[k], pair_recv.at[k], s, partner
+        )
+
+    def sum_copy(k, row_from, row_to):
+        return put(
+            middle.at[k], arrived.at[row_from],
+            sum_send.at[k], sum_recv.at[0], s, 2 * row_to + half,
         )
 
     def fine_sums():
         grads = matmul_nt(fine_x[...], fine_cols[:, plane:plane + own]).astype(BF)
-        for j in range(OWNERS):
+        for j in range(KEEPERS):
             parts[j] = grads[j * share:(j + 1) * share, :]
-        for j in range(OWNERS):
-            @pl.when(v != first_owner + j)
-            def _(j=j):
-                sum_copy(j, v, first_owner + j).start()
-
-            @pl.when(v == first_owner + j)
-            def _(j=j):
-                arrived[v] = parts[j]
+
+    def pair_sends():
+        for k in range(2):
+            pair_copy(k).start()
+
+    def part_rows(part):
+        return pl.ds(part * rows_each, rows_each)
+
+    def straight_copy(j, part, vol_to):
+        return put(
+            parts.at[j, part_rows(part)], landed.at[part, v],
+            straight_send.at[0], straight_recv.at[part], s, vol_to,
+        )
+
+    def straight_landed(part):
+        block = landed.at[part, pl.ds(0, n - 1)]
+        return put(block, block, straight_send.at[0], straight_recv.at[part], s, partner)
+
+    def straight_sends():
+        def send(order):
+            for part in range(PARTS):
+                for j in order:
+                    @pl.when(v != first_keeper + j)
+                    def _(j=j, part=part):
+                        straight_copy(j, part, first_keeper + j).start()
+
+        @pl.when(v < n // 2)
+        def _():
+            send(range(KEEPERS - 1, -1, -1))
+
+        @pl.when(v >= n // 2)
+        def _():
+            send(range(KEEPERS))
+
+        @pl.when(keeper)
+        def _():
+            for part in range(PARTS):
+                landed[part, v] = parts[mine, part_rows(part)]
+
+    def column_sums():
+        for k in range(2):
+            pair_copy(k).wait_recv()
+            both = parts[2 * half + k].astype(F32) + paired[k].astype(F32)
+            middle[k] = both.astype(BF)
+
+            @pl.when(row != first_owner + k)
+            def _(k=k):
+                sum_copy(k, row, first_owner + k).start()
+
+            @pl.when(row == first_owner + k)
+            def _(k=k):
+                arrived[row] = middle[k]
 
     @pl.when(s == 0)
     def _():
         fine_sums()
+        straight_sends()
+        send_gz()
+
+    @pl.when(last)
+    def _():
+        copies = step_copies(seed, 0, s)
+        on_left(wait_send, copies[1], copies[3])
+        on_right(wait_send, copies[2], copies[4])
 
     outgoing = step_copies(out, 1, s - 1)
     terms = matmul(fine_cat[...], fine_cols[...])
@@ -467,39 +546,58 @@
 
     @pl.when(s > 0)
     def _():
-        outgoing[5].start()
+        outgoing[6].start()
         pool_out[1] = pool_of(out)
         on_left(start, outgoing[1])
         on_right(start, outgoing[2])
         outgoing[0].start()
         on_left(start, outgoing[3])
         on_right(start, outgoing[4])
-        for p in range(1, depth):
-            outgoing[5 + p].start()
+        outgoing[7].start()
+
+    @pl.when(s == segments - 2)
+    def _():
+        credit(s + 1)
 
     @pl.when(last)
     def _():
         pl.semaphore_wait(go, 1)
+
+    @pl.when(late)
+    def _():
         on_left(start, x_left)
         on_right(start, x_right)
-
-    @pl.when(late)
-    def _():
         send_rows(1)
         take_pooled()
-
-    @pl.when(last)
-    def _():
         on_left(wait_recv, x_right)
         on_right(wait_recv, x_left)
         take_fine_x()
 
+    @pl.when(late)
+    def _():
+        send_gz()
+
     @pl.when(s > 0)
     def _():
         fine_sums()
-        send_rows(2)
+
+        @pl.when(paced)
+        def _():
+            pair_sends()
+
+        @pl.when(direct)
+        def _():
+            straight_sends()
+
+    grad_store = pltpu.make_async_copy(grad_out, grad_o, store_sem.at[0])
+    coarse_store = pltpu.make_async_copy(coarse_out, coarse_o, store_sem.at[1])
+
+    def fine_store(outer, first, stop):
+        at = (slice(outer * 9, (outer + 1) * 9), slice(first, stop))
+        return pltpu.make_async_copy(fine_out.at[at], fine_o.at[at], store_sem.at[2])
 
     grad_out[...] = jnp.swapaxes(out[...], 0, 1)
+    grad_store.start()
 
     def coarse_sums():
         total = jnp.zeros((3 * channels, 9 * channels), F32)
@@ -536,72 +634,140 @@
                 ]
             at += count
 
-    def all_copy(j, off, vol_to):
+    @pl.when(paced)
+    def _():
+        column_sums()
+
+    def hand_copy(piece, row_to):
         return put(
-            collected.at[j], collected.at[j], all_send.at[off], all_recv.at[j], s, vol_to
-        )
-
-    @pl.when(owner)
-    def _():
-        def arrive(off, carry):
-            u = lax.rem(v + off, n)
-            sum_copy(0, u, u).wait_recv()
+            collected.at[piece], collected.at[piece],
+            hand_send.at[0], all_recv.at[piece], s, 2 * row_to + half,
+        )
+
+    def pass_copy(k, piece):
+        return put(
+            collected.at[piece], collected.at[piece],
+            pass_send.at[k], all_recv.at[piece], s, partner,
+        )
+
+    def other_rows(act):
+        def body(off, carry):
+            act(lax.rem(row + off, columns))
             return carry
 
-        lax.fori_loop(1, n, arrive, 0)
-        whole = arrived[0].astype(F32)
-        for u in range(1, n):
-            whole = whole + arrived[u].astype(F32)
-        collected[mine] = whole.astype(BF)
-
-        def hand(off, carry):
-            all_copy(mine, off, lax.rem(v + off, n)).start()
-            return carry
-
-        lax.fori_loop(1, n, hand, 0)
+        lax.fori_loop(1, columns, body, 0)
+
+    sums_arrived = put(
+        arrived.at[pl.ds(0, columns - 1)], arrived.at[pl.ds(0, columns - 1)],
+        sum_send.at[0], sum_recv.at[0], s, partner,
+    )
+
+    for k in range(2):
+        @pl.when((row == first_owner + k) & paced)
+        def _(k=k):
+            piece = 2 * half + k
+            sums_arrived.wait_recv()
+            whole = arrived[0].astype(F32)
+            for u in range(1, columns):
+                whole = whole + arrived[u].astype(F32)
+            collected[piece] = whole.astype(BF)
+            other_rows(lambda u: hand_copy(piece, u).start())
+            pass_copy(k, piece).start()
+
+    def spread_copy(j, part, vol_to):
+        block = collected.at[j, part_rows(part)]
+        return put(block, block, spread_send.at[0], all_recv.at[j], s, vol_to)
+
+    def whole_share(j):
+        return put(
+            collected.at[j], collected.at[j], spread_send.at[0], all_recv.at[j], s, partner
+        )
+
+    @pl.when(keeper & direct)
+    def _():
+        for part in range(PARTS):
+            straight_landed(part).wait_recv()
+            whole = landed[part, 0].astype(F32)
+            for u in range(1, n):
+                whole = whole + landed[part, u].astype(F32)
+            collected[mine, part_rows(part)] = whole.astype(BF)
+            far_first(lambda u, part=part: spread_copy(mine, part, u).start())
 
     wait_rows(2)
     place(coarse_out, 0, coarse_sums())
-
-    for j in range(OWNERS):
-        @pl.when(v != first_owner + j)
-        def _(j=j):
-            all_copy(j, 0, v).wait_recv()
-
-        place(fine_out, j * share, collected[j].astype(F32) * scales[0])
-
-    def rest(off, carry):
-        for which in range(3):
-            row_copy(which, off).wait_send()
-
-        @pl.when(owner)
+    coarse_store.start()
+
+    for which in range(3):
+        all_rows(which).wait_send()
+
+    @pl.when(paced)
+    def _():
+        for k in range(2):
+            pair_copy(k).wait_send()
+
+            @pl.when(row != first_owner + k)
+            def _(k=k):
+                sum_copy(k, row, first_owner + k).wait_send()
+
+    @pl.when(direct)
+    def _():
+        @pl.when(keeper)
         def _():
-            all_copy(mine, off, lax.rem(v + off, n)).wait_send()
-
-        return carry
-
-    lax.fori_loop(1, n, rest, 0)
-    for j in range(OWNERS):
-        @pl.when(v != first_owner + j)
-        def _(j=j):
-            sum_copy(j, v, first_owner + j).wait_send()
+            block = parts.at[pl.ds(0, KEEPERS - 1)]
+            put(block, block, straight_send.at[0], straight_recv.at[0], s, partner).wait_send()
+
+        @pl.when(jnp.logical_not(keeper))
+        def _():
+            put(parts, parts, straight_send.at[0], straight_recv.at[0], s, partner).wait_send()
 
     on_left(wait_send, pre_left, x_left)
     on_right(wait_send, pre_right, x_right)
-
-    @pl.when(last)
-    def _():
-        copies = step_copies(seed, 0, s)
-        on_left(wait_send, copies[1], copies[3])
-        on_right(wait_send, copies[2], copies[4])
 
     @pl.when(s > 0)
     def _():
         on_left(wait_send, outgoing[1], outgoing[3])
         on_right(wait_send, outgoing[2], outgoing[4])
         wait_send(outgoing[0])
-        for p in range(depth):
-            wait_send(outgoing[5 + p])
+        wait_send(outgoing[5])
+
+    @pl.when(paced)
+    def _():
+        for k in range(2):
+            @pl.when(row != first_owner + k)
+            def _(k=k):
+                hand_copy(2 * half + k, row).wait_recv()
+                pass_copy(k, 2 * half + k).start()
+
+        for k in range(2):
+            pass_copy(k, 2 * other + k).wait_recv()
+
+    for j in range(KEEPERS):
+        @pl.when(direct & (v != first_keeper + j))
+        def _(j=j):
+            whole_share(j).wait_recv()
+
+        place(fine_out, j * share, collected[j].astype(F32) * scales[0])
+        for outer in range(j * share // channels, ((j + 1) * share - 1) // channels + 1):
+            first = max(j * share, outer * channels) - outer * channels
+            stop = min((j + 1) * share, (outer + 1) * channels) - outer * channels
+            fine_store(outer, first, stop).start()
+
+    @pl.when(paced)
+    def _():
+        for k in range(2):
+            pass_copy(k, 2 * half + k).wait_send()
+
+            @pl.when(row == first_owner + k)
+            def _(k=k):
+                other_rows(lambda u: hand_copy(2 * half + k, u).wait_send())
+
+    @pl.when(keeper & direct)
+    def _():
+        others(lambda u: whole_share(mine).wait_send())
+
+    grad_store.wait()
+    coarse_store.wait()
+    pltpu.make_async_copy(fine_out, fine_o, store_sem.at[2]).wait()
 
 
 def finish(grad, fine, coarse, grad_out, fine_out, coarse_out, sem):
@@ -635,11 +801,11 @@
     sizes = (segments, n, channels, depth, plane)
     group = min(GROUP_LANES, n * slab)
     groups = n * slab // group
-    share = 3 * channels // OWNERS
+    share = (3 * channels // KEEPERS, 9 * channels)
     pick_shape = (n * row_len, reach * cw)
     if math.prod(pick_shape) * 2 > PICK_BYTES:
         pick_shape = (1, 128)
-    vmem = pl.BlockSpec(memory_space=pltpu.VMEM)
+    spaces = pl.BlockSpec(memory_space=pl.ANY)
     limit = min(60 * MIB, 16 * MIB + 6 * 2 * 9 * channels * (own + 2 * plane))
     hbm = pl.BlockSpec(memory_space=pltpu.HBM)
     dma = pltpu.SemaphoreType.DMA
@@ -649,15 +815,17 @@
         functools.partial(kernel, sizes, scales),
         out_shape=(grad_shape, tap_shape, tap_shape),
         in_specs=[hbm] * 9,
-        out_specs=(vmem, vmem, vmem),
+        out_specs=(spaces, spaces, spaces),
         scratch_shapes=[
+            pltpu.VMEM((channels, depth, plane), BF),
+            pltpu.VMEM((TAPS, channels, channels), F32),
+            pltpu.VMEM((TAPS, channels, channels), F32),
             pltpu.SMEM(class_weight.shape, F32),
             pltpu.VMEM(cotangent.shape, BF),
             pltpu.VMEM(labels.shape, jnp.int32),
             pltpu.VMEM((channels, depth, plane), BF),
             pltpu.VMEM((channels, depth, plane), BF),
-            pltpu.VMEM((TAPS, channels, channels), BF),
-            pltpu.VMEM((TAPS, channels, channels), BF),
+            pltpu.VMEM((2, TAPS, channels, channels), BF),
             pltpu.VMEM((depth, channels, plane), BF),
             pltpu.VMEM((depth, channels, plane), BF),
             pltpu.VMEM((3 * channels, 9 * channels), BF),
@@ -671,19 +839,22 @@
             pltpu.VMEM((2, channels, slab), BF),
             pltpu.VMEM((channels, reach * cw), BF),
             pltpu.VMEM(pick_shape, BF),
-            pltpu.VMEM((slab, own), BF),
+            pltpu.VMEM((own, slab), BF),
             pltpu.VMEM((3 * channels, own), BF),
             pltpu.VMEM((groups, channels, group), BF),
             pltpu.VMEM((9 * channels, own + 2 * plane), BF),
             pltpu.VMEM((9 * channels, reach * cw), BF),
             pltpu.VMEM((9 * channels, group), BF),
             pltpu.VMEM((n, channels, slab), BF),
-            pltpu.VMEM((OWNERS, share, 9 * channels), BF),
-            pltpu.VMEM((n, share, 9 * channels), BF),
-            pltpu.VMEM((OWNERS, share, 9 * channels), BF),
-            dma((9,)), dma((3, n)), dma((3, n)), dma((4,)), dma((4,)),
-            dma((2, 5 + depth)), dma((5 + depth,)),
-            dma((OWNERS,)), dma((n,)), dma((n,)), dma((OWNERS,)), dma((1,)), dma((1,)),
+            pltpu.VMEM((KEEPERS, *share), BF),
+            pltpu.VMEM((PARTS, n, share[0] // PARTS, share[1]), BF),
+            pltpu.VMEM((2, *share), BF),
+            pltpu.VMEM((2, *share), BF),
+            pltpu.VMEM((n // 2, *share), BF),
+            pltpu.VMEM((KEEPERS, *share), BF),
+            dma((8,)), dma((3,)), dma((3,)), dma((4,)), dma((4,)), dma((6,)), dma((6,)),
+            dma((2,)), dma((2,)), dma((2,)), dma((1,)), dma((1,)), dma((2,)), dma((KEEPERS,)),
+            dma((1,)), dma((PARTS,)), dma((1,)), dma((3,)),
             pltpu.SemaphoreType.REGULAR,
         ],
         compiler_params=pltpu.CompilerParams(
@@ -706,7 +877,6 @@
         )
     )
 
-    spaces = pl.BlockSpec(memory_space=pl.ANY)
     grad, fine_grads, coarse_grads = pl.pallas_call(
         finish,
         out_shape=(grad_shape, tap_shape, tap_shape),

time: 44.7 us -> 41 us (0.917)
  Pallas kernels: 43.9 us -> 40.2 us
    pallas_call x1, Pallas kernels: 42.7 us -> 38.9 us  [on_device(): pl.pallas_call(functools.partial(kernel, sizes, scales), out_shape=(grad_...]
where the time goes in v2:
time: 41 us; the launch traced here: 40.8 us
  Pallas kernels  40.2 us (98%)
  between operations  0.64 us (2%)
    pallas_call x1, Pallas kernels, on_device(): pl.pallas_call(functools.partial(kernel, sizes, scales), out_shape=(grad_...  38.9 us
    pallas_call x1, Pallas kernels, on_device(): pl.pallas_call(finish, out_shape=(grad_shape, tap_shape, tap_shape), in_s...  1.27 us

profile of v2, /device:TPU:0, one launch (start us, length us, event | category | flops | bytes accessed | tf_op | source)
XLA Modules:
  0.0 40.8 jit_solution(1684431927583630120)
XLA Ops:
  0.6 38.9 %shard_map.112 = (bf16[64,4,256]{2,1,0:T(4,128)(2,1)S(1)}, f32[27,64,64]{2,1,0:T(8,128)S(1)}, f32[27,64,64]{2,1,0:T(8,128)S(1)}) custom-call(f32[3]{0:T(128)} %class_weight_h.1, bf16[64,4,256]{2,1,0:T(4,128)(2,1)} %cotangent_h.1, s32[4,256]{1,0:T(4,128)} %labels_h.1, bf16[64,4,256]{2,1,0:T(4,128)(2,1)} %bitcast.11, bf16[64,4,256]{2,1,0:T(4,128)(2,1)} %bitcast.12, ...), custom_call_target="tpu_custom_call" | custom-call | tf_op jit(solution)/shard_map/pallas_call | solution.py:814
  39.6 1.3 %shard_map.113 = (bf16[64,4,256]{2,1,0:T(4,128)(2,1)}, f32[27,64,64]{2,1,0:T(8,128)}, f32[27,64,64]{2,1,0:T(8,128)}) custom-call(bf16[64,4,256]{2,1,0:T(4,128)(2,1)S(1)} %get-tuple-element.9.grad, f32[27,64,64]{2,1,0:T(8,128)S(1)} %get-tuple-element.10.fine, f32[27,64,64]{2,1,0:T(8,128)S(1)} %get-tuple-element.11.coarse), custom_call_target="tpu_custom_call" | custom-call | tf_op jit(solution)/shard_map/pallas_call | solution.py:880

commit v3 on v2

--- a/solution.py
+++ b/solution.py
@@ -57,7 +57,7 @@
     grad_o, fine_o, coarse_o,
     grad_out, fine_out, coarse_out, class_weight, cotangent, labels, saved, fine_pre, weights,
     out, seed, fine_cat, coarse_cat, pre_rows, pool_rows, pre_ext, x_ext, grad_ext, pool_ext,
-    pool_out, coarse_gate, pick, pool_matrix, fine_x, pool_all, fine_cols, coarse_cols,
+    pool_out, coarse_gate, pick, pool_matrix, up_matrix, fine_x, pool_all, fine_cols, coarse_cols,
     full_cols, gz_all, parts, landed, paired, middle, arrived, collected,
     load_sem, row_send, row_recv, halo_send, halo_recv, step_send, step_recv,
     pair_send, pair_recv, sum_send, sum_recv, hand_send, pass_send, all_recv,
@@ -156,9 +156,16 @@
     )
     pool_matrix[...] = jnp.where(iota((own, slab), 1) == pool_target, 1.0, 0.0).astype(BF)
 
-    up_lane = iota((1, plane), 1)
-    up_target = lax.div(up_lane, 2 * XL) * HX + lax.div(lax.rem(up_lane, XL), 2)
-    up_matrix = jnp.where(iota((cw, plane), 0) == up_target, 0.125, 0.0).astype(BF)
+    up_wide = (cdepth + 2) * plane
+    up_lane = iota((1, up_wide), 1)
+    up_target = (
+        lax.div(up_lane, plane) * cw
+        + lax.div(lax.rem(up_lane, plane), 2 * XL) * HX
+        + lax.div(lax.rem(up_lane, XL), 2)
+    )
+    up_matrix[...] = jnp.where(
+        iota(((cdepth + 2) * cw, up_wide), 0) == up_target, 0.125, 0.0
+    ).astype(BF)
 
     reach = cdepth + 4
     reach_lane = iota((1, reach * cw), 1)
@@ -291,6 +298,16 @@
 
         lax.fori_loop(1, n, body, 0)
 
+    def in_order(act):
+        def body(u, carry):
+            @pl.when(u != v)
+            def _():
+                act(u)
+
+            return carry
+
+        lax.fori_loop(0, n, body, 0)
+
     def others(act):
         def body(off, carry):
             act(lax.rem(v + off, n))
@@ -403,6 +420,10 @@
     def _():
         incoming[0].wait_recv()
 
+    @pl.when(s == segments - 2)
+    def _():
+        credit(s + 1)
+
     side = pool_ext.shape[2]
     near = jnp.concatenate(
         [pool_ext[0][:, side - 2 * cw:], pool_ext[1], pool_ext[2][:, :2 * cw]], axis=1
@@ -422,14 +443,10 @@
         for outer in range(3)
     ).astype(BF)
 
-    pieces = []
-    for p in range(depth + 2):
-        j = (p + 1) // 2
-        if p and j == p // 2:
-            spread = pieces[-1]
-        else:
-            spread = matmul(coarse_back[:, j * cw:(j + 1) * cw], up_matrix)
-        pieces.append(spread)
+    spread = matmul(coarse_back, up_matrix[...])
+    pieces = [
+        spread[:, (p + 1) // 2 * plane:((p + 1) // 2 + 1) * plane] for p in range(depth + 2)
+    ]
 
     on_left(wait_recv, pre_right, incoming[4])
     on_right(wait_recv, pre_left, incoming[3])
@@ -442,16 +459,26 @@
     def _():
         send_gz()
 
-    gz = []
-    for p in range(depth + 2):
-        grad = grad_ext[p].astype(F32) + pieces[p]
-        gz.append(jnp.where(pre_ext[p].astype(F32) > 0, grad, 0.0).astype(BF))
-    for r, (row_step, col_step) in enumerate(STEPS):
-        mask = tap_mask(plane, plane, XL, row_step, col_step)
+    def take_cols():
+        masks = [tap_mask(plane, plane, XL, *step) for step in STEPS]
         for p in range(depth + 2):
-            fine_cols[r * channels:(r + 1) * channels, p * plane:(p + 1) * plane] = (
-                rolled(gz[p], row_step * XL + col_step) * mask
-            )
+            grad = grad_ext[p].astype(F32) + pieces[p]
+            gz = jnp.where(pre_ext[p].astype(F32) > 0, grad, 0.0).astype(BF)
+            for r, (row_step, col_step) in enumerate(STEPS):
+                fine_cols[r * channels:(r + 1) * channels, p * plane:(p + 1) * plane] = (
+                    rolled(gz, row_step * XL + col_step) * masks[r]
+                )
+
+    def take_out():
+        terms = matmul(fine_cat[...], fine_cols[...])
+        for p in range(depth):
+            total = grad_ext[p + 1].astype(F32)
+            for outer in range(3):
+                total = total + terms[
+                    outer * channels:(outer + 1) * channels,
+                    (p + 2 - outer) * plane:(p + 3 - outer) * plane,
+                ]
+            out[p] = total.astype(BF)
 
     def pair_copy(k):
         return put(
@@ -464,10 +491,11 @@
             sum_send.at[k], sum_recv.at[0], s, 2 * row_to + half,
         )
 
-    def fine_sums():
-        grads = matmul_nt(fine_x[...], fine_cols[:, plane:plane + own]).astype(BF)
-        for j in range(KEEPERS):
-            parts[j] = grads[j * share:(j + 1) * share, :]
+    def fine_sums(first, count):
+        rows = slice(first * share, (first + count) * share)
+        grads = matmul_nt(fine_x[rows, :], fine_cols[:, plane:plane + own]).astype(BF)
+        for j in range(count):
+            parts[first + j] = grads[j * share:(j + 1) * share, :]
 
     def pair_sends():
         for k in range(2):
@@ -486,7 +514,9 @@
         block = landed.at[part, pl.ds(0, n - 1)]
         return put(block, block, straight_send.at[0], straight_recv.at[part], s, partner)
 
-    def straight_sends():
+    def straight_sums():
+        fine_sums(0, KEEPERS)
+
         def send(order):
             for part in range(PARTS):
                 for j in order:
@@ -502,7 +532,7 @@
         def _():
             send(range(KEEPERS))
 
-        @pl.when(keeper)
+        @pl.when((mine >= 0) & (mine < KEEPERS))
         def _():
             for part in range(PARTS):
                 landed[part, v] = parts[mine, part_rows(part)]
@@ -523,9 +553,12 @@
 
     @pl.when(s == 0)
     def _():
-        fine_sums()
-        straight_sends()
+        take_cols()
+        straight_sums()
         send_gz()
+        take_out()
+
+    outgoing = step_copies(out, 1, s - 1)
 
     @pl.when(last)
     def _():
@@ -533,19 +566,10 @@
         on_left(wait_send, copies[1], copies[3])
         on_right(wait_send, copies[2], copies[4])
 
-    outgoing = step_copies(out, 1, s - 1)
-    terms = matmul(fine_cat[...], fine_cols[...])
-    for p in range(depth):
-        total = grad_ext[p + 1].astype(F32)
-        for outer in range(3):
-            total = total + terms[
-                outer * channels:(outer + 1) * channels,
-                (p + 2 - outer) * plane:(p + 3 - outer) * plane,
-            ]
-        out[p] = total.astype(BF)
-
     @pl.when(s > 0)
     def _():
+        take_cols()
+        take_out()
         outgoing[6].start()
         pool_out[1] = pool_of(out)
         on_left(start, outgoing[1])
@@ -555,10 +579,6 @@
         on_right(start, outgoing[4])
         outgoing[7].start()
 
-    @pl.when(s == segments - 2)
-    def _():
-        credit(s + 1)
-
     @pl.when(last)
     def _():
         pl.semaphore_wait(go, 1)
@@ -568,6 +588,9 @@
         on_left(start, x_left)
         on_right(start, x_right)
         send_rows(1)
+
+    @pl.when(late)
+    def _():
         take_pooled()
         on_left(wait_recv, x_right)
         on_right(wait_recv, x_left)
@@ -579,15 +602,14 @@
 
     @pl.when(s > 0)
     def _():
-        fine_sums()
-
         @pl.when(paced)
         def _():
+            fine_sums(0, KEEPERS)
             pair_sends()
 
         @pl.when(direct)
         def _():
-            straight_sends()
+            straight_sums()
 
     grad_store = pltpu.make_async_copy(grad_out, grad_o, store_sem.at[0])
     coarse_store = pltpu.make_async_copy(coarse_out, coarse_o, store_sem.at[1])
@@ -691,7 +713,7 @@
             for u in range(1, n):
                 whole = whole + landed[part, u].astype(F32)
             collected[mine, part_rows(part)] = whole.astype(BF)
-            far_first(lambda u, part=part: spread_copy(mine, part, u).start())
+            in_order(lambda u, part=part: spread_copy(mine, part, u).start())
 
     wait_rows(2)
     place(coarse_out, 0, coarse_sums())
@@ -840,6 +862,7 @@
             pltpu.VMEM((channels, reach * cw), BF),
             pltpu.VMEM(pick_shape, BF),
             pltpu.VMEM((own, slab), BF),
+            pltpu.VMEM(((cdepth + 2) * cw, (cdepth + 2) * plane), BF),
             pltpu.VMEM((3 * channels, own), BF),
             pltpu.VMEM((groups, channels, group), BF),
             pltpu.VMEM((9 * channels, own + 2 * plane), BF),

time: 41 us -> 39.3 us (0.959)
  Pallas kernels: 40.2 us -> 38.5 us
    pallas_call x1, Pallas kernels: 38.9 us -> 37.2 us  [on_device(): pl.pallas_call(functools.partial(kernel, sizes, scales), out_shape=(grad_...]
where the time goes in v3:
time: 39.3 us; the launch traced here: 39.1 us
  Pallas kernels  38.5 us (98%)
  between operations  0.64 us (2%)
    pallas_call x1, Pallas kernels, on_device(): pl.pallas_call(functools.partial(kernel, sizes, scales), out_shape=(grad_...  37.2 us
    pallas_call x1, Pallas kernels, on_device(): pl.pallas_call(finish, out_shape=(grad_shape, tap_shape, tap_shape), in_s...  1.27 us

profile of v3, /device:TPU:0, one launch (start us, length us, event | category | flops | bytes accessed | tf_op | source)
XLA Modules:
  0.0 39.1 jit_solution(15456862526449380911)
XLA Ops:
  0.6 37.2 %shard_map.112 = (bf16[64,4,256]{2,1,0:T(4,128)(2,1)S(1)}, f32[27,64,64]{2,1,0:T(8,128)S(1)}, f32[27,64,64]{2,1,0:T(8,128)S(1)}) custom-call(f32[3]{0:T(128)} %class_weight_h.1, bf16[64,4,256]{2,1,0:T(4,128)(2,1)} %cotangent_h.1, s32[4,256]{1,0:T(4,128)} %labels_h.1, bf16[64,4,256]{2,1,0:T(4,128)(2,1)} %bitcast.11, bf16[64,4,256]{2,1,0:T(4,128)(2,1)} %bitcast.12, ...), custom_call_target="tpu_custom_call" | custom-call | tf_op jit(solution)/shard_map/pallas_call | solution.py:836
  37.9 1.3 %shard_map.113 = (bf16[64,4,256]{2,1,0:T(4,128)(2,1)}, f32[27,64,64]{2,1,0:T(8,128)}, f32[27,64,64]{2,1,0:T(8,128)}) custom-call(bf16[64,4,256]{2,1,0:T(4,128)(2,1)S(1)} %get-tuple-element.9.grad, f32[27,64,64]{2,1,0:T(8,128)S(1)} %get-tuple-element.10.fine, f32[27,64,64]{2,1,0:T(8,128)S(1)} %get-tuple-element.11.coarse), custom_call_target="tpu_custom_call" | custom-call | tf_op jit(solution)/shard_map/pallas_call | solution.py:903

commit v4 on v3

--- a/solution.py
+++ b/solution.py
@@ -56,7 +56,7 @@
     fine_w_h, coarse_w_h,
     grad_o, fine_o, coarse_o,
     grad_out, fine_out, coarse_out, class_weight, cotangent, labels, saved, fine_pre, weights,
-    out, seed, fine_cat, coarse_cat, pre_rows, pool_rows, pre_ext, x_ext, grad_ext, pool_ext,
+    out, seed, fine_cat, coarse_cat, own_rows, to_send, pre_rows, pool_rows, pre_ext, x_ext, grad_ext, pool_ext,
     pool_out, coarse_gate, pick, pool_matrix, up_matrix, fine_x, pool_all, fine_cols, coarse_cols,
     full_cols, gz_all, parts, landed, paired, middle, arrived, collected,
     load_sem, row_send, row_recv, halo_send, halo_recv, step_send, step_recv,
@@ -84,8 +84,9 @@
     row = lax.div(v, 2)
     columns = n // 2
     first_owner = columns // 2 - 1
-    share = 3 * channels // KEEPERS
-    rows_each = share // PARTS
+    share = channels // KEEPERS
+    tiles = parts.shape[2] // 128
+    cuts = [128 * (tiles * part // PARTS) for part in range(PARTS + 1)]
     first_keeper = n // 2 - KEEPERS // 2
     mine = v - first_keeper
     keeper = (mine >= 0) & (mine < KEEPERS)
@@ -125,7 +126,8 @@
     def load(src, dst, index):
         return pltpu.make_async_copy(src, dst, load_sem.at[index])
 
-    rows_load = load(coarse_pre_h, pre_rows.at[v], 0)
+    compact = pick.shape[0] > 1
+    rows_load = load(coarse_pre_h, own_rows if compact else pre_rows.at[v], 0)
     pre_load = load(fine_pre_h, fine_pre, 1)
     seed_loads = (
         load(class_weight_h, class_weight, 2),
@@ -156,17 +158,6 @@
     )
     pool_matrix[...] = jnp.where(iota((own, slab), 1) == pool_target, 1.0, 0.0).astype(BF)
 
-    up_wide = (cdepth + 2) * plane
-    up_lane = iota((1, up_wide), 1)
-    up_target = (
-        lax.div(up_lane, plane) * cw
-        + lax.div(lax.rem(up_lane, plane), 2 * XL) * HX
-        + lax.div(lax.rem(up_lane, XL), 2)
-    )
-    up_matrix[...] = jnp.where(
-        iota(((cdepth + 2) * cw, up_wide), 0) == up_target, 0.125, 0.0
-    ).astype(BF)
-
     reach = cdepth + 4
     reach_lane = iota((1, reach * cw), 1)
     reach_depth = v * cdepth - 2 + lax.div(reach_lane, cw)
@@ -175,16 +166,23 @@
         (reach_depth >= 0) & (reach_depth < n * cdepth), reach_cell, -1
     )
     reach_inline = lax.div(lax.rem(reach_lane, cw), HX)
-    whole_pick = pick.shape[0] > 1
 
     def picked(rows, u, cell, inline, lanes):
         chosen = iota((row_len, lanes), 0) == jnp.where(inline == u, cell, -1)
         return matmul(rows[u], jnp.where(chosen, 1.0, 0.0).astype(BF))
 
-    if whole_pick:
-        for u in range(n):
-            chosen = iota((row_len, reach * cw), 0) == jnp.where(reach_inline == u, reach_cell, -1)
-            pick[u * row_len:(u + 1) * row_len, :] = jnp.where(chosen, 1.0, 0.0).astype(BF)
+    small = channels // 2
+    if compact:
+        to_lane = iota((1, n * 128), 1)
+        to_cell = lax.rem(to_lane, 128 // 2)
+        to_depth = lax.div(to_lane, 128) * cdepth - 2 + lax.div(to_cell, HX)
+        to_row = (
+            lax.div(lax.rem(to_lane, 128), 128 // 2) * row_len
+            + to_depth * HX + lax.rem(to_cell, HX)
+        )
+        inside = (to_depth >= 0) & (to_depth < n * cdepth) & (to_cell < reach * HX)
+        to_row = jnp.where(inside, to_row, -1)
+        split = jnp.where(iota((2 * row_len, n * 128), 0) == to_row, 1.0, 0.0).astype(BF)
 
     def step_copies(src, turn, segment):
         def step(which, a, b, vol):
@@ -270,6 +268,12 @@
 
     rows_load.wait()
     pooled_load.wait()
+    if compact:
+        halves = jnp.concatenate([own_rows[:small, :], own_rows[small:, :]], axis=1)
+        blocks = matmul(halves, split).astype(BF)
+        for u in range(n):
+            to_send[u] = blocks[:, u * 128:(u + 1) * 128]
+        pre_rows[v] = to_send[v]
 
     ups = jnp.where(s > 0, 1, 0) + jnp.where(last, 0, 1)
     sides = 1 + jnp.where(has_left, 1, 0) + jnp.where(has_right, 1, 0)
@@ -317,8 +321,10 @@
 
     def row_copy(which, source, target):
         ref = (pre_rows, pool_rows, gz_all)[which]
+        compacted = compact and which == 0
         return put(
-            ref.at[source], ref.at[source], row_send.at[which], row_recv.at[which], s, target
+            to_send.at[target] if compacted else ref.at[source], ref.at[source],
+            row_send.at[which], row_recv.at[which], s, target,
         )
 
     def all_rows(which):
@@ -359,15 +365,37 @@
         on_left(start, x_left)
         on_right(start, x_right)
 
+    up_wide = (cdepth + 2) * plane
+    up_lane = iota((1, up_wide), 1)
+    up_target = (
+        lax.div(up_lane, plane) * cw
+        + lax.div(lax.rem(up_lane, plane), 2 * XL) * HX
+        + lax.div(lax.rem(up_lane, XL), 2)
+    )
+    up_matrix[...] = jnp.where(
+        iota(((cdepth + 2) * cw, up_wide), 0) == up_target, 0.125, 0.0
+    ).astype(BF)
+
+    if compact:
+        for u in range(n):
+            from_row = iota((128, 2 * reach * cw), 0)
+            to_lane = lax.rem(iota((1, 2 * reach * cw), 1), reach * cw)
+            second = lax.div(iota((1, 2 * reach * cw), 1), reach * cw)
+            wanted = second * (128 // 2) + lax.div(to_lane, cw) * HX + lax.rem(to_lane, HX)
+            wanted = jnp.where(lax.div(lax.rem(to_lane, cw), HX) == u, wanted, -1)
+            pick[u * 128:(u + 1) * 128, :] = jnp.where(from_row == wanted, 1.0, 0.0).astype(BF)
+
     wait_rows(0)
 
     @pl.when(last)
     def _():
         credit(s - 1)
 
-    if whole_pick:
+    if compact:
         flat_rows = jnp.concatenate([pre_rows[u] for u in range(n)], axis=1)
-        coarse_gate[...] = matmul(flat_rows, pick[...]).astype(BF)
+        gates = matmul(flat_rows, pick[...]).astype(BF)
+        coarse_gate[:small, :] = gates[:, :reach * cw]
+        coarse_gate[small:, :] = gates[:, reach * cw:]
     else:
         coarse_gate[...] = lax.fori_loop(
             0, n,
@@ -394,10 +422,12 @@
         lax.fori_loop(0, groups, body, 0)
 
     def take_fine_x():
-        for outer in range(3):
+        for block in range(9):
+            outer, row_step = block // 3, 1 - block % 3
+            mask = tap_mask(plane, plane, XL, row_step, 0)
             for p in range(depth):
-                fine_x[outer * channels:(outer + 1) * channels, p * plane:(p + 1) * plane] = (
-                    x_ext[p + outer]
+                fine_x[block * channels:(block + 1) * channels, p * plane:(p + 1) * plane] = (
+                    rolled(x_ext[p + outer], row_step * XL) * mask
                 )
 
     @pl.when(jnp.logical_not(late))
@@ -459,14 +489,15 @@
     def _():
         send_gz()
 
-    def take_cols():
-        masks = [tap_mask(plane, plane, XL, *step) for step in STEPS]
-        for p in range(depth + 2):
+    def take_cols(planes, first, count):
+        for p in planes:
             grad = grad_ext[p].astype(F32) + pieces[p]
             gz = jnp.where(pre_ext[p].astype(F32) > 0, grad, 0.0).astype(BF)
-            for r, (row_step, col_step) in enumerate(STEPS):
+            for r in range(first, first + count):
+                row_step, col_step = STEPS[r]
+                mask = tap_mask(plane, plane, XL, row_step, col_step)
                 fine_cols[r * channels:(r + 1) * channels, p * plane:(p + 1) * plane] = (
-                    rolled(gz, row_step * XL + col_step) * masks[r]
+                    rolled(gz, row_step * XL + col_step) * mask
                 )
 
     def take_out():
@@ -491,31 +522,36 @@
             sum_send.at[k], sum_recv.at[0], s, 2 * row_to + half,
         )
 
-    def fine_sums(first, count):
-        rows = slice(first * share, (first + count) * share)
-        grads = matmul_nt(fine_x[rows, :], fine_cols[:, plane:plane + own]).astype(BF)
-        for j in range(count):
-            parts[first + j] = grads[j * share:(j + 1) * share, :]
+    def fine_sums():
+        gz = fine_cols[3 * channels:6 * channels, plane:plane + own]
+        grads = matmul_nt(fine_x[...], gz)
+        blocks = [grads[block * channels:(block + 1) * channels, :] for block in range(9)]
+        rest = parts.shape[2] - TAPS * channels
+        if rest:
+            blocks.append(jnp.zeros((channels, rest), F32))
+        flat = jnp.concatenate(blocks, axis=1).astype(BF)
+        for j in range(KEEPERS):
+            parts[j] = flat[j * share:(j + 1) * share, :]
 
     def pair_sends():
         for k in range(2):
             pair_copy(k).start()
 
-    def part_rows(part):
-        return pl.ds(part * rows_each, rows_each)
+    def lanes_of(part):
+        return slice(cuts[part], cuts[part + 1])
 
     def straight_copy(j, part, vol_to):
         return put(
-            parts.at[j, part_rows(part)], landed.at[part, v],
+            parts.at[j, :, lanes_of(part)], landed.at[v, :, lanes_of(part)],
             straight_send.at[0], straight_recv.at[part], s, vol_to,
         )
 
     def straight_landed(part):
-        block = landed.at[part, pl.ds(0, n - 1)]
+        block = landed.at[pl.ds(0, n - 1), :, lanes_of(part)]
         return put(block, block, straight_send.at[0], straight_recv.at[part], s, partner)
 
     def straight_sums():
-        fine_sums(0, KEEPERS)
+        fine_sums()
 
         def send(order):
             for part in range(PARTS):
@@ -534,8 +570,7 @@
 
         @pl.when((mine >= 0) & (mine < KEEPERS))
         def _():
-            for part in range(PARTS):
-                landed[part, v] = parts[mine, part_rows(part)]
+            landed[v] = parts[mine]
 
     def column_sums():
         for k in range(2):
@@ -553,9 +588,13 @@
 
     @pl.when(s == 0)
     def _():
-        take_cols()
+        inner = range(1, depth + 1)
+        take_cols(inner, 3, 3)
         straight_sums()
         send_gz()
+        take_cols(inner, 0, 3)
+        take_cols(inner, 6, 3)
+        take_cols((0, depth + 1), 0, 9)
         take_out()
 
     outgoing = step_copies(out, 1, s - 1)
@@ -568,7 +607,7 @@
 
     @pl.when(s > 0)
     def _():
-        take_cols()
+        take_cols(range(depth + 2), 0, 9)
         take_out()
         outgoing[6].start()
         pool_out[1] = pool_of(out)
@@ -604,7 +643,7 @@
     def _():
         @pl.when(paced)
         def _():
-            fine_sums(0, KEEPERS)
+            fine_sums()
             pair_sends()
 
         @pl.when(direct)
@@ -614,9 +653,10 @@
     grad_store = pltpu.make_async_copy(grad_out, grad_o, store_sem.at[0])
     coarse_store = pltpu.make_async_copy(coarse_out, coarse_o, store_sem.at[1])
 
-    def fine_store(outer, first, stop):
-        at = (slice(outer * 9, (outer + 1) * 9), slice(first, stop))
-        return pltpu.make_async_copy(fine_out.at[at], fine_o.at[at], store_sem.at[2])
+    def fine_store(rows):
+        return pltpu.make_async_copy(
+            fine_out.at[:, rows], fine_o.at[:, rows], store_sem.at[2]
+        )
 
     grad_out[...] = jnp.swapaxes(out[...], 0, 1)
     grad_store.start()
@@ -697,7 +737,7 @@
             pass_copy(k, piece).start()
 
     def spread_copy(j, part, vol_to):
-        block = collected.at[j, part_rows(part)]
+        block = collected.at[j, :, lanes_of(part)]
         return put(block, block, spread_send.at[0], all_recv.at[j], s, vol_to)
 
     def whole_share(j):
@@ -709,10 +749,11 @@
     def _():
         for part in range(PARTS):
             straight_landed(part).wait_recv()
-            whole = landed[part, 0].astype(F32)
+            at = lanes_of(part)
+            whole = landed[0, :, at].astype(F32)
             for u in range(1, n):
-                whole = whole + landed[part, u].astype(F32)
-            collected[mine, part_rows(part)] = whole.astype(BF)
+                whole = whole + landed[u, :, at].astype(F32)
+            collected[mine, :, at] = whole.astype(BF)
             in_order(lambda u, part=part: spread_copy(mine, part, u).start())
 
     wait_rows(2)
@@ -768,11 +809,11 @@
         def _(j=j):
             whole_share(j).wait_recv()
 
-        place(fine_out, j * share, collected[j].astype(F32) * scales[0])
-        for outer in range(j * share // channels, ((j + 1) * share - 1) // channels + 1):
-            first = max(j * share, outer * channels) - outer * channels
-            stop = min((j + 1) * share, (outer + 1) * channels) - outer * channels
-            fine_store(outer, first, stop).start()
+        value = collected[j].astype(F32) * scales[0]
+        rows = slice(j * share, (j + 1) * share)
+        for k in range(TAPS):
+            fine_out[k, rows, :] = value[:, k * channels:(k + 1) * channels]
+        fine_store(rows).start()
 
     @pl.when(paced)
     def _():
@@ -823,10 +864,12 @@
     sizes = (segments, n, channels, depth, plane)
     group = min(GROUP_LANES, n * slab)
     groups = n * slab // group
-    share = (3 * channels // KEEPERS, 9 * channels)
-    pick_shape = (n * row_len, reach * cw)
-    if math.prod(pick_shape) * 2 > PICK_BYTES:
+    share = (channels // KEEPERS, -(-TAPS * channels // 128) * 128)
+    pick_shape = (n * 128, 2 * reach * cw)
+    compact_shape = (channels // 2, 128)
+    if math.prod(pick_shape) * 2 > PICK_BYTES or reach * HX > 64:
         pick_shape = (1, 128)
+        compact_shape = (channels, row_len)
     spaces = pl.BlockSpec(memory_space=pl.ANY)
     limit = min(60 * MIB, 16 * MIB + 6 * 2 * 9 * channels * (own + 2 * plane))
     hbm = pl.BlockSpec(memory_space=pltpu.HBM)
@@ -852,7 +895,9 @@
             pltpu.VMEM((depth, channels, plane), BF),
             pltpu.VMEM((3 * channels, 9 * channels), BF),
             pltpu.VMEM((3 * channels, 9 * channels), BF),
-            pltpu.VMEM((n, channels, row_len), BF),
+            pltpu.VMEM((channels, row_len), BF),
+            pltpu.VMEM((n, channels // 2, 128), BF),
+            pltpu.VMEM((n, *compact_shape), BF),
             pltpu.VMEM((n, channels, row_len), BF),
             pltpu.VMEM((depth + 2, channels, plane), BF),
             pltpu.VMEM((depth + 2, channels, plane), BF),
@@ -863,14 +908,14 @@
             pltpu.VMEM(pick_shape, BF),
             pltpu.VMEM((own, slab), BF),
             pltpu.VMEM(((cdepth + 2) * cw, (cdepth + 2) * plane), BF),
-            pltpu.VMEM((3 * channels, own), BF),
+            pltpu.VMEM((9 * channels, own), BF),
             pltpu.VMEM((groups, channels, group), BF),
             pltpu.VMEM((9 * channels, own + 2 * plane), BF),
             pltpu.VMEM((9 * channels, reach * cw), BF),
             pltpu.VMEM((9 * channels, group), BF),
             pltpu.VMEM((n, channels, slab), BF),
             pltpu.VMEM((KEEPERS, *share), BF),
-            pltpu.VMEM((PARTS, n, share[0] // PARTS, share[1]), BF),
+            pltpu.VMEM((n, *share), BF),
             pltpu.VMEM((2, *share), BF),
             pltpu.VMEM((2, *share), BF),
             pltpu.VMEM((n // 2, *share), BF),

time: 39.3 us -> 38.8 us (0.987)
  Pallas kernels: 38.5 us -> 38 us
    pallas_call x1, Pallas kernels: 37.2 us -> 36.7 us  [on_device(): pl.pallas_call(functools.partial(kernel, sizes, scales), out_shape=(grad_...]
where the time goes in v4:
time: 38.8 us; the launch traced here: 38.6 us
  Pallas kernels  38 us (98%)
  between operations  0.64 us (2%)
    pallas_call x1, Pallas kernels, on_device(): pl.pallas_call(functools.partial(kernel, sizes, scales), out_shape=(grad_...  36.7 us
    pallas_call x1, Pallas kernels, on_device(): pl.pallas_call(finish, out_shape=(grad_shape, tap_shape, tap_shape), in_s...  1.27 us

profile of v4, /device:TPU:0, one launch (start us, length us, event | category | flops | bytes accessed | tf_op | source)
XLA Modules:
  0.0 38.6 jit_solution(5010444104345657698)
XLA Ops:
  0.6 36.7 %shard_map.112 = (bf16[64,4,256]{2,1,0:T(4,128)(2,1)S(1)}, f32[27,64,64]{2,1,0:T(8,128)S(1)}, f32[27,64,64]{2,1,0:T(8,128)S(1)}) custom-call(f32[3]{0:T(128)} %class_weight_h.1, bf16[64,4,256]{2,1,0:T(4,128)(2,1)} %cotangent_h.1, s32[4,256]{1,0:T(4,128)} %labels_h.1, bf16[64,4,256]{2,1,0:T(4,128)(2,1)} %bitcast.11, bf16[64,4,256]{2,1,0:T(4,128)(2,1)} %bitcast.12, ...), custom_call_target="tpu_custom_call" | custom-call | tf_op jit(solution)/shard_map/pallas_call | solution.py:879
  37.4 1.3 %shard_map.113 = (bf16[64,4,256]{2,1,0:T(4,128)(2,1)}, f32[27,64,64]{2,1,0:T(8,128)}, f32[27,64,64]{2,1,0:T(8,128)}) custom-call(bf16[64,4,256]{2,1,0:T(4,128)(2,1)S(1)} %get-tuple-element.9.grad, f32[27,64,64]{2,1,0:T(8,128)S(1)} %get-tuple-element.10.fine, f32[27,64,64]{2,1,0:T(8,128)S(1)} %get-tuple-element.11.coarse), custom_call_target="tpu_custom_call" | custom-call | tf_op jit(solution)/shard_map/pallas_call | solution.py:948

commit v5 on v4

--- a/solution.py
+++ b/solution.py
@@ -60,8 +60,8 @@
     pool_out, coarse_gate, pick, pool_matrix, up_matrix, fine_x, pool_all, fine_cols, coarse_cols,
     full_cols, gz_all, parts, landed, paired, middle, arrived, collected,
     load_sem, row_send, row_recv, halo_send, halo_recv, step_send, step_recv,
-    pair_send, pair_recv, sum_send, sum_recv, hand_send, pass_send, all_recv,
-    straight_send, straight_recv, spread_send, store_sem, go,
+    pair_recv, sum_send, sum_recv, all_recv,
+    straight_recv, go,
 ):
     segments, n, channels, depth, plane = sizes
     cw = plane // 4
@@ -76,7 +76,7 @@
     has_left, has_right = v > 0, v < n - 1
     last = s == segments - 1
     late = s >= segments - 2
-    paced = lax.rem(s, 2) == 1
+    paced = (lax.rem(s, 2) == 1) & (s < segments - 1)
     direct = jnp.logical_not(paced)
     half = lax.rem(v, 2)
     other = 1 - half
@@ -150,14 +150,6 @@
     for copy in (pre_load, coarse_w_load, fine_w_load, saved_load, pooled_load):
         copy.start()
 
-    fine_lane = iota((own, 1), 0)
-    pool_target = (
-        lax.div(fine_lane, 2 * plane) * cw
-        + lax.div(lax.rem(fine_lane, plane), 2 * XL) * HX
-        + lax.div(lax.rem(fine_lane, XL), 2)
-    )
-    pool_matrix[...] = jnp.where(iota((own, slab), 1) == pool_target, 1.0, 0.0).astype(BF)
-
     reach = cdepth + 4
     reach_lane = iota((1, reach * cw), 1)
     reach_depth = v * cdepth - 2 + lax.div(reach_lane, cw)
@@ -225,49 +217,61 @@
         flat = jnp.concatenate([ref[p] for p in range(depth)], axis=1)
         return matmul(flat, pool_matrix[...]).astype(BF)
 
-    @pl.when(last)
-    def _():
-        for copy in seed_loads:
-            copy.wait()
-        planes = jnp.swapaxes(cotangent[...], 0, 1)
-        for p in range(depth):
-            label = labels[p:p + 1, :]
-            weight = jnp.zeros(label.shape, F32)
-            for index in range(class_weight.shape[0]):
-                weight = weight + jnp.where(label == index, class_weight[index], 0.0)
-            block = (planes[p].astype(F32) * weight).astype(BF)
-            seed[p] = block
-            grad_ext[p + 1] = block
-        pool_out[0] = pool_of(seed)
-        pool_ext[1] = pool_out[0]
-
-    pre_load.wait()
-    pre_ext[1:depth + 1] = jnp.swapaxes(fine_pre[...], 0, 1)
-    both_w_load.wait()
-    for k in range(TAPS):
-        rows = slice(k // 9 * channels, (k // 9 + 1) * channels)
-        lanes = slice(k % 9 * channels, (k % 9 + 1) * channels)
-        coarse_cat[rows, lanes] = weights[0, k]
-        fine_cat[rows, lanes] = weights[1, k]
-    saved_load.wait()
-    x_ext[1:depth + 1] = jnp.swapaxes(saved[...], 0, 1)
-
-    @pl.when(v == 0)
-    def _():
-        pre_ext[0] = jnp.zeros((channels, plane), BF)
-        x_ext[0] = jnp.zeros((channels, plane), BF)
-        grad_ext[0] = jnp.zeros((channels, plane), BF)
-        pool_ext[0] = jnp.zeros(pool_ext.shape[1:], BF)
-
-    @pl.when(v == n - 1)
-    def _():
-        pre_ext[depth + 1] = jnp.zeros((channels, plane), BF)
-        x_ext[depth + 1] = jnp.zeros((channels, plane), BF)
-        grad_ext[depth + 1] = jnp.zeros((channels, plane), BF)
-        pool_ext[2] = jnp.zeros(pool_ext.shape[1:], BF)
+    def prepare():
+        fine_lane = iota((own, 1), 0)
+        pool_target = (
+            lax.div(fine_lane, 2 * plane) * cw
+            + lax.div(lax.rem(fine_lane, plane), 2 * XL) * HX
+            + lax.div(lax.rem(fine_lane, XL), 2)
+        )
+        pool_matrix[...] = jnp.where(iota((own, slab), 1) == pool_target, 1.0, 0.0).astype(BF)
+
+        @pl.when(last)
+        def _():
+            for copy in seed_loads:
+                copy.wait()
+            planes = jnp.swapaxes(cotangent[...], 0, 1)
+            for p in range(depth):
+                label = labels[p:p + 1, :]
+                weight = jnp.zeros(label.shape, F32)
+                for index in range(class_weight.shape[0]):
+                    weight = weight + jnp.where(label == index, class_weight[index], 0.0)
+                block = (planes[p].astype(F32) * weight).astype(BF)
+                seed[p] = block
+                grad_ext[p + 1] = block
+            pool_out[0] = pool_of(seed)
+            pool_ext[1] = pool_out[0]
+
+        pre_load.wait()
+        pre_ext[1:depth + 1] = jnp.swapaxes(fine_pre[...], 0, 1)
+        both_w_load.wait()
+        for k in range(TAPS):
+            rows = slice(k // 9 * channels, (k // 9 + 1) * channels)
+            lanes = slice(k % 9 * channels, (k % 9 + 1) * channels)
+            coarse_cat[rows, lanes] = weights[0, k]
+            fine_cat[rows, lanes] = weights[1, k]
+        saved_load.wait()
+        x_ext[1:depth + 1] = jnp.swapaxes(saved[...], 0, 1)
+
+        @pl.when(v == 0)
+        def _():
+            pre_ext[0] = jnp.zeros((channels, plane), BF)
+            x_ext[0] = jnp.zeros((channels, plane), BF)
+            grad_ext[0] = jnp.zeros((channels, plane), BF)
+            pool_ext[0] = jnp.zeros(pool_ext.shape[1:], BF)
+
+        @pl.when(v == n - 1)
+        def _():
+            pre_ext[depth + 1] = jnp.zeros((channels, plane), BF)
+            x_ext[depth + 1] = jnp.zeros((channels, plane), BF)
+            grad_ext[depth + 1] = jnp.zeros((channels, plane), BF)
+            pool_ext[2] = jnp.zeros(pool_ext.shape[1:], BF)
+
+        pooled_load.wait()
+
+    pl.when(v < n // 2)(prepare)
 
     rows_load.wait()
-    pooled_load.wait()
     if compact:
         halves = jnp.concatenate([own_rows[:small, :], own_rows[small:, :]], axis=1)
         blocks = matmul(halves, split).astype(BF)
@@ -343,10 +347,15 @@
 
     @pl.when(last)
     def _():
+        send_rows(0)
+
+    pl.when(v >= n // 2)(prepare)
+
+    @pl.when(last)
+    def _():
         copies = step_copies(seed, 0, s)
         on_left(start, copies[1])
         on_right(start, copies[2])
-        send_rows(0)
         on_left(start, copies[3], pre_left)
         on_right(start, copies[4], pre_right)
 
@@ -377,13 +386,13 @@
     ).astype(BF)
 
     if compact:
+        from_row = iota((128 // 2, reach * cw), 0)
+        to_lane = iota((1, reach * cw), 1)
+        wanted = lax.div(to_lane, cw) * HX + lax.rem(to_lane, HX)
+        to_inline = lax.div(lax.rem(to_lane, cw), HX)
         for u in range(n):
-            from_row = iota((128, 2 * reach * cw), 0)
-            to_lane = lax.rem(iota((1, 2 * reach * cw), 1), reach * cw)
-            second = lax.div(iota((1, 2 * reach * cw), 1), reach * cw)
-            wanted = second * (128 // 2) + lax.div(to_lane, cw) * HX + lax.rem(to_lane, HX)
-            wanted = jnp.where(lax.div(lax.rem(to_lane, cw), HX) == u, wanted, -1)
-            pick[u * 128:(u + 1) * 128, :] = jnp.where(from_row == wanted, 1.0, 0.0).astype(BF)
+            chosen = from_row == jnp.where(to_inline == u, wanted, -1)
+            pick[u * 64:(u + 1) * 64, :] = jnp.where(chosen, 1.0, 0.0).astype(BF)
 
     wait_rows(0)
 
@@ -392,10 +401,15 @@
         credit(s - 1)
 
     if compact:
-        flat_rows = jnp.concatenate([pre_rows[u] for u in range(n)], axis=1)
-        gates = matmul(flat_rows, pick[...]).astype(BF)
-        coarse_gate[:small, :] = gates[:, :reach * cw]
-        coarse_gate[small:, :] = gates[:, reach * cw:]
+        arrivals = [pre_rows[u] for u in range(n)]
+        flat_rows = jnp.concatenate(
+            [
+                jnp.concatenate([rows[:, 64 * h:64 * (h + 1)] for rows in arrivals], axis=1)
+                for h in range(2)
+            ],
+            axis=0,
+        )
+        coarse_gate[...] = matmul(flat_rows, pick[...]).astype(BF)
     else:
         coarse_gate[...] = lax.fori_loop(
             0, n,
@@ -513,7 +527,7 @@
 
     def pair_copy(k):
         return put(
-            parts.at[2 * other + k], paired.at[k], pair_send.at[k], pair_recv.at[k], s, partner
+            parts.at[2 * other + k], paired.at[k], load_sem.at[3 + k], pair_recv.at[k], s, partner
         )
 
     def sum_copy(k, row_from, row_to):
@@ -543,12 +557,12 @@
     def straight_copy(j, part, vol_to):
         return put(
             parts.at[j, :, lanes_of(part)], landed.at[v, :, lanes_of(part)],
-            straight_send.at[0], straight_recv.at[part], s, vol_to,
+            load_sem.at[3], straight_recv.at[part], s, vol_to,
         )
 
     def straight_landed(part):
         block = landed.at[pl.ds(0, n - 1), :, lanes_of(part)]
-        return put(block, block, straight_send.at[0], straight_recv.at[part], s, partner)
+        return put(block, block, load_sem.at[3], straight_recv.at[part], s, partner)
 
     def straight_sums():
         fine_sums()
@@ -650,12 +664,12 @@
         def _():
             straight_sums()
 
-    grad_store = pltpu.make_async_copy(grad_out, grad_o, store_sem.at[0])
-    coarse_store = pltpu.make_async_copy(coarse_out, coarse_o, store_sem.at[1])
+    grad_store = pltpu.make_async_copy(grad_out, grad_o, load_sem.at[0])
+    coarse_store = pltpu.make_async_copy(coarse_out, coarse_o, load_sem.at[1])
 
     def fine_store(rows):
         return pltpu.make_async_copy(
-            fine_out.at[:, rows], fine_o.at[:, rows], store_sem.at[2]
+            fine_out.at[:, rows], fine_o.at[:, rows], load_sem.at[2]
         )
 
     grad_out[...] = jnp.swapaxes(out[...], 0, 1)
@@ -703,13 +717,13 @@
     def hand_copy(piece, row_to):
         return put(
             collected.at[piece], collected.at[piece],
-            hand_send.at[0], all_recv.at[piece], s, 2 * row_to + half,
+            load_sem.at[5], all_recv.at[piece], s, 2 * row_to + half,
         )
 
     def pass_copy(k, piece):
         return put(
             collected.at[piece], collected.at[piece],
-            pass_send.at[k], all_recv.at[piece], s, partner,
+            load_sem.at[6 + k], all_recv.at[piece], s, partner,
         )
 
     def other_rows(act):
@@ -738,11 +752,11 @@
 
     def spread_copy(j, part, vol_to):
         block = collected.at[j, :, lanes_of(part)]
-        return put(block, block, spread_send.at[0], all_recv.at[j], s, vol_to)
+        return put(block, block, load_sem.at[5], all_recv.at[j], s, vol_to)
 
     def whole_share(j):
         return put(
-            collected.at[j], collected.at[j], spread_send.at[0], all_recv.at[j], s, partner
+            collected.at[j], collected.at[j], load_sem.at[5], all_recv.at[j], s, partner
         )
 
     @pl.when(keeper & direct)
@@ -777,11 +791,11 @@
         @pl.when(keeper)
         def _():
             block = parts.at[pl.ds(0, KEEPERS - 1)]
-            put(block, block, straight_send.at[0], straight_recv.at[0], s, partner).wait_send()
+            put(block, block, load_sem.at[3], straight_recv.at[0], s, partner).wait_send()
 
         @pl.when(jnp.logical_not(keeper))
         def _():
-            put(parts, parts, straight_send.at[0], straight_recv.at[0], s, partner).wait_send()
+            put(parts, parts, load_sem.at[3], straight_recv.at[0], s, partner).wait_send()
 
     on_left(wait_send, pre_left, x_left)
     on_right(wait_send, pre_right, x_right)
@@ -830,7 +844,7 @@
 
     grad_store.wait()
     coarse_store.wait()
-    pltpu.make_async_copy(fine_out, fine_o, store_sem.at[2]).wait()
+    pltpu.make_async_copy(fine_out, fine_o, load_sem.at[2]).wait()
 
 
 def finish(grad, fine, coarse, grad_out, fine_out, coarse_out, sem):
@@ -865,7 +879,7 @@
     group = min(GROUP_LANES, n * slab)
     groups = n * slab // group
     share = (channels // KEEPERS, -(-TAPS * channels // 128) * 128)
-    pick_shape = (n * 128, 2 * reach * cw)
+    pick_shape = (n * 64, reach * cw)
     compact_shape = (channels // 2, 128)
     if math.prod(pick_shape) * 2 > PICK_BYTES or reach * HX > 64:
         pick_shape = (1, 128)
@@ -921,8 +935,7 @@
             pltpu.VMEM((n // 2, *share), BF),
             pltpu.VMEM((KEEPERS, *share), BF),
             dma((8,)), dma((3,)), dma((3,)), dma((4,)), dma((4,)), dma((6,)), dma((6,)),
-            dma((2,)), dma((2,)), dma((2,)), dma((1,)), dma((1,)), dma((2,)), dma((KEEPERS,)),
-            dma((1,)), dma((PARTS,)), dma((1,)), dma((3,)),
+            dma((2,)), dma((2,)), dma((1,)), dma((KEEPERS,)), dma((PARTS,)),
             pltpu.SemaphoreType.REGULAR,
         ],
         compiler_params=pltpu.CompilerParams(

time: 38.8 us -> 38.2 us (0.985)
  Pallas kernels: 38 us -> 37.4 us
    pallas_call x1, Pallas kernels: 36.7 us -> 36.2 us  [on_device(): pl.pallas_call(functools.partial(kernel, sizes, scales), out_shape=(grad_...]
where the time goes in v5:
time: 38.2 us; the launch traced here: 38.1 us
  Pallas kernels  37.4 us (98%)
  between operations  0.64 us (2%)
    pallas_call x1, Pallas kernels, on_device(): pl.pallas_call(functools.partial(kernel, sizes, scales), out_shape=(grad_...  36.2 us
    pallas_call x1, Pallas kernels, on_device(): pl.pallas_call(finish, out_shape=(grad_shape, tap_shape, tap_shape), in_s...  1.27 us

profile of v5, /device:TPU:0, one launch (start us, length us, event | category | flops | bytes accessed | tf_op | source)
XLA Modules:
  0.0 38.1 jit_solution(7765259740242492975)
XLA Ops:
  0.6 36.2 %shard_map.112 = (bf16[64,4,256]{2,1,0:T(4,128)(2,1)S(1)}, f32[27,64,64]{2,1,0:T(8,128)S(1)}, f32[27,64,64]{2,1,0:T(8,128)S(1)}) custom-call(f32[3]{0:T(128)} %class_weight_h.1, bf16[64,4,256]{2,1,0:T(4,128)(2,1)} %cotangent_h.1, s32[4,256]{1,0:T(4,128)} %labels_h.1, bf16[64,4,256]{2,1,0:T(4,128)(2,1)} %bitcast.11, bf16[64,4,256]{2,1,0:T(4,128)(2,1)} %bitcast.12, ...), custom_call_target="tpu_custom_call" | custom-call | tf_op jit(solution)/shard_map/pallas_call | solution.py:893
  36.8 1.3 %shard_map.113 = (bf16[64,4,256]{2,1,0:T(4,128)(2,1)}, f32[27,64,64]{2,1,0:T(8,128)}, f32[27,64,64]{2,1,0:T(8,128)}) custom-call(bf16[64,4,256]{2,1,0:T(4,128)(2,1)S(1)} %get-tuple-element.9.grad, f32[27,64,64]{2,1,0:T(8,128)S(1)} %get-tuple-element.10.fine, f32[27,64,64]{2,1,0:T(8,128)S(1)} %get-tuple-element.11.coarse), custom_call_target="tpu_custom_call" | custom-call | tf_op jit(solution)/shard_map/pallas_call | solution.py:961

commit v6 on v5

--- a/solution.py
+++ b/solution.py
@@ -338,9 +338,37 @@
     def send_rows(which):
         far_first(lambda u: row_copy(which, v, u).start())
 
+    def gz_copy(source, recv, target):
+        block = gz_all.at[source]
+        return put(block, block, row_send.at[2], row_recv.at[recv], s, target)
+
     def send_gz():
-        for off in range(1, n):
-            row_copy(2, v, lax.rem(v + off, n)).start()
+        @pl.when(direct)
+        def _():
+            for off in range(1, n):
+                gz_copy(v, 2, lax.rem(v + off, n)).start()
+
+        @pl.when(paced)
+        def _():
+            for off in range(1, columns):
+                gz_copy(v, 2, 2 * lax.rem(row + off, columns) + half).start()
+            gz_copy(v, 3, partner).start()
+
+    def pass_gz():
+        block = gz_all.at[pl.ds(0, columns - 1)]
+        put(block, block, row_send.at[2], row_recv.at[2], s, partner).wait_recv()
+        for off in range(1, columns):
+            gz_copy(2 * lax.rem(row + off, columns) + half, 3, partner).start()
+
+    def wait_gz():
+        @pl.when(direct)
+        def _():
+            all_rows(2).wait_recv()
+
+        @pl.when(paced)
+        def _():
+            block = gz_all.at[pl.ds(0, columns)]
+            put(block, block, row_send.at[2], row_recv.at[3], s, partner).wait_recv()
 
     def wait_rows(which):
         all_rows(which).wait_recv()
@@ -712,6 +740,7 @@
 
     @pl.when(paced)
     def _():
+        pass_gz()
         column_sums()
 
     def hand_copy(piece, row_to):
@@ -770,7 +799,7 @@
             collected[mine, :, at] = whole.astype(BF)
             in_order(lambda u, part=part: spread_copy(mine, part, u).start())
 
-    wait_rows(2)
+    wait_gz()
     place(coarse_out, 0, coarse_sums())
     coarse_store.start()
 
@@ -934,7 +963,7 @@
             pltpu.VMEM((2, *share), BF),
             pltpu.VMEM((n // 2, *share), BF),
             pltpu.VMEM((KEEPERS, *share), BF),
-            dma((8,)), dma((3,)), dma((3,)), dma((4,)), dma((4,)), dma((6,)), dma((6,)),
+            dma((8,)), dma((3,)), dma((4,)), dma((4,)), dma((4,)), dma((6,)), dma((6,)),
             dma((2,)), dma((2,)), dma((1,)), dma((KEEPERS,)), dma((PARTS,)),
             pltpu.SemaphoreType.REGULAR,
         ],

time: 38.2 us -> 38.1 us (level)
  no operation moved by 1% of the time
where the time goes in v6:
time: 38.1 us; the launch traced here: 38 us
  Pallas kernels  37.3 us (98%)
  between operations  0.64 us (2%)
    pallas_call x1, Pallas kernels, on_device(): pl.pallas_call(functools.partial(kernel, sizes, scales), out_shape=(grad_...  36 us
    pallas_call x1, Pallas kernels, on_device(): pl.pallas_call(finish, out_shape=(grad_shape, tap_shape, tap_shape), in_s...  1.27 us

profile of v6, /device:TPU:0, one launch (start us, length us, event | category | flops | bytes accessed | tf_op | source)
XLA Modules:
  0.0 38.0 jit_solution(8370753627379555963)
XLA Ops:
  0.6 36.0 %shard_map.112 = (bf16[64,4,256]{2,1,0:T(4,128)(2,1)S(1)}, f32[27,64,64]{2,1,0:T(8,128)S(1)}, f32[27,64,64]{2,1,0:T(8,128)S(1)}) custom-call(f32[3]{0:T(128)} %class_weight_h.1, bf16[64,4,256]{2,1,0:T(4,128)(2,1)} %cotangent_h.1, s32[4,256]{1,0:T(4,128)} %labels_h.1, bf16[64,4,256]{2,1,0:T(4,128)(2,1)} %bitcast.11, bf16[64,4,256]{2,1,0:T(4,128)(2,1)} %bitcast.12, ...), custom_call_target="tpu_custom_call" | custom-call | tf_op jit(solution)/shard_map/pallas_call | solution.py:922
  36.7 1.3 %shard_map.113 = (bf16[64,4,256]{2,1,0:T(4,128)(2,1)}, f32[27,64,64]{2,1,0:T(8,128)}, f32[27,64,64]{2,1,0:T(8,128)}) custom-call(bf16[64,4,256]{2,1,0:T(4,128)(2,1)S(1)} %get-tuple-element.9.grad, f32[27,64,64]{2,1,0:T(8,128)S(1)} %get-tuple-element.10.fine, f32[27,64,64]{2,1,0:T(8,128)S(1)} %get-tuple-element.11.coarse), custom_call_target="tpu_custom_call" | custom-call | tf_op jit(solution)/shard_map/pallas_call | solution.py:990
